TPU v7x, 256 devices: a whole 4x4x8 slice. The times are simulated.
256 devices in a mesh: tm: 16 (over z, core), space: 16 (over x, y).
Axes of the slice: x: 4, y: 4, z: 8, core: 2. Of those that a mesh axis runs over, the one named last changes fastest.
Arguments:
- concentration: float32 [4, 16, 1024, 2048], P(None, 'tm', 'space'), may hold values from -5.5 to 5.5
- forcing: float32 [4, 16, 1024, 2048], P(None, 'tm', 'space'), may hold values from -5.5 to 5.5
- eigenbasis: bfloat16 [2048, 2048], replicated, may hold values from -0.125 to 0.125
- eigenvalues: float32 [2048], replicated, may hold values from -0.5 to -0.001, as said below
- settle_table: float32 [8], replicated, may hold values from 0.002 to 0.5, as said below
- fraction_class: int32 [4], replicated, may hold values from 0 to 7
- bed_mask: int32 [1024, 2048], P('space'), may hold values 0 or 1
Outputs:
- updated: float32 [4, 16, 1024, 2048], P(None, 'tm', 'space')
Inputs may be any that keep to these rules, and one draw needn't show every extreme that they name: `fraction_class`: index into settle_table. `bed_mask`: 1 marks a bed cell. `eigenvalues`: negative. `settle_table`: positive.
All inputs are finite; a program needn't handle non-finite values. No bound on the sum of `bed_mask` on one device may be relied on, other than what follows from the above.
Results may differ from a plain program's by a relative error of at most 0.0055.
Values may be sent and summed in bfloat16 or wider, within the bound.
A program may use at most 64 MiB of HBM per device.

v0:
```python
import math

import jax
import jax.numpy as jnp
from jax import lax
from jax.sharding import PartitionSpec as P

CIRCULANT_ALPHA = 0.5
VERTICAL_DIFFUSION = 0.06
DEPOSITION = 0.1


def extended(block, sides, width):
    for axis, dim in sides:
        count = lax.axis_size(axis)
        forward = [(i, i + 1) for i in range(count - 1)]
        backward = [(target, source) for source, target in forward]
        low = lax.ppermute(
            lax.slice_in_dim(block, block.shape[dim] - width, None, axis=dim), axis, forward
        )
        high = lax.ppermute(lax.slice_in_dim(block, 0, width, axis=dim), axis, backward)
        block = jnp.concatenate([low, block, high], axis=dim)
    return block


def from_behind(value, axis, steps):
    count = lax.axis_size(axis)
    initial, last = (max(0, -steps), min(count, count - steps))
    return lax.ppermute(value, axis, [(source, source + steps) for source in range(initial, last)])


def twiddles(first_index, second_index, length):
    products = first_index[:, None] * second_index[None, :] % length
    angle_grid = 2.0 * math.pi / length * products.astype(jnp.float32)
    return (jnp.cos(angle_grid), jnp.sin(angle_grid))


def apply_table(table, values):
    return jnp.einsum(
        "kn,fnrx->fkrx", table, values.astype(jnp.float32), precision=lax.Precision.HIGHEST
    )


def to_space(modal, eigenbasis):
    return lax.dot_general(
        modal, eigenbasis, (((1,), (1,)), ((), ())), preferred_element_type=jnp.float32
    )


def solve_shifted(
    real_part, imag_part, freq_index, length, decay_ratio, eigenbasis, eigenvalues, diagonal
):
    layout = real_part.shape
    columns = layout[-1]
    stacked = (
        jnp.concatenate([real_part, imag_part], axis=0).astype(jnp.bfloat16).reshape(-1, columns)
    )
    modal = jnp.dot(stacked, eigenbasis, preferred_element_type=jnp.float32).reshape((2,) + layout)
    angles = 2.0 * math.pi / length * freq_index.astype(jnp.float32)
    shift_real = (
        (1.0 - decay_ratio * jnp.cos(angles))[None, :, None, None]
        - eigenvalues[None, None, None, :]
        + diagonal[:, None, None, None]
    )
    shift_imag = (decay_ratio * jnp.sin(angles))[None, :, None, None]
    magnitude = shift_real * shift_real + shift_imag * shift_imag
    scaled_real = (modal[0] * shift_real + modal[1] * shift_imag) / magnitude
    scaled_imag = (modal[1] * shift_real - modal[0] * shift_imag) / magnitude
    scaled = (
        jnp.concatenate([scaled_real, scaled_imag], axis=0)
        .astype(jnp.bfloat16)
        .reshape(-1, columns)
    )
    back = to_space(scaled, eigenbasis).astype(jnp.bfloat16).reshape((2,) + layout)
    return (back[0], back[1])


def on_device(
    concentration, forcing, eigenbasis, eigenvalues, settle_table, fraction_class, bed_mask
):
    fractions, slices, row_count, columns = concentration.shape
    tm_devices = lax.axis_size("tm")
    length = slices * tm_devices
    classes = settle_table.shape[0]
    onehot = (fraction_class[:, None] == jnp.arange(classes, dtype=jnp.int32)[None, :]).astype(
        jnp.float32
    )
    settling = jnp.sum(onehot * settle_table[None, :], axis=1)
    diagonal = 2.0 * VERTICAL_DIFFUSION + settling
    decay_ratio = CIRCULANT_ALPHA ** (1.0 / length)
    first_slice = lax.axis_index("tm") * slices
    slice_index = first_slice + jnp.arange(slices, dtype=jnp.int32)
    slice_times = slice_index.astype(jnp.float32)
    scale_up = decay_ratio**slice_times
    scale_down = decay_ratio ** (-slice_times)
    bed_cells = bed_mask.astype(jnp.float32)
    padded = extended(concentration, (("space", 2),), 1)
    upper_row = padded[:, :, :-2]
    lower_row = padded[:, :, 2:]
    vertical = (
        VERTICAL_DIFFUSION * (lower_row - 2.0 * concentration + upper_row)
        + settling[:, None, None, None] * (upper_row - concentration)
        - DEPOSITION * bed_cells[None, None] * concentration
    )
    coupled = (
        jnp.dot(
            concentration.astype(jnp.bfloat16).reshape(-1, columns),
            eigenbasis,
            preferred_element_type=jnp.float32,
        )
        * eigenvalues[None, :]
    ).astype(jnp.bfloat16)
    along_x = to_space(coupled, eigenbasis).reshape(concentration.shape)
    last_slice = from_behind(concentration, "tm", 1)
    earlier = jnp.concatenate([last_slice, concentration[:, : slices - 1]], axis=1)
    residual = forcing - (concentration - along_x - vertical - earlier)
    scaled = (scale_up[None, :, None, None] * residual).astype(jnp.bfloat16)
    by_rows = lax.all_to_all(scaled, "tm", split_axis=2, concat_axis=1, tiled=True)
    all_index = jnp.arange(length, dtype=jnp.int32)
    cosine_table, sine_table = twiddles(all_index, all_index, length)
    real_part = apply_table(cosine_table, by_rows)
    imag_part = -apply_table(sine_table, by_rows)
    back_real, back_imag = solve_shifted(
        real_part, imag_part, all_index, length, decay_ratio, eigenbasis, eigenvalues, diagonal
    )
    relaxed_rows = (
        apply_table(cosine_table, back_real) - apply_table(sine_table, back_imag)
    ) / length
    relaxed = lax.all_to_all(relaxed_rows, "tm", split_axis=1, concat_axis=2, tiled=True)
    return concentration + scale_down[None, :, None, None] * relaxed


def solution(mesh):
    return jax.shard_map(
        on_device,
        mesh=mesh,
        in_specs=(
            P(None, "tm", "space", None),
            P(None, "tm", "space", None),
            P(),
            P(),
            P(),
            P(),
            P("space", None),
        ),
        out_specs=P(None, "tm", "space", None),
        check_vma=False,
    )
```

profile of v0, /device:TPU:1, one launch (start us, length us, event | category | flops | bytes accessed | tf_op | source)
XLA Modules:
  0.0 189.0 jit_solution(3372452159803485570)
XLA Ops:
  0.0 0.0 copy-start.3
  0.0 5.0 %collective-permute-start.2 = (f32[4,1,64,2048]{3,2,1,0:T(8,128)}, f32[4,1,64,2048]{3,2,1,0:T(8,128)}, u32[]{:S(2)}, u32[]{:S(2)}) collective-permute-start(f32[4,1,64,2048]{3,2,1,0:T(8,128)} %param.7), channel_id=1, source_target_pairs={{0,16},{16,32},{32,48},{48,64},{64,80},{80,96},{96,112},{112,128},... | collective-permute-start | bytes 6291464 | tf_op jit(solution)/shard_map/ppermute | solution.py:29
  5.1 1.1 fusion.61
  6.1 1.3 collective-permute-start
  7.4 0.0 copy-start.4
  7.5 4.0 %collective-permute-start.1 = (f32[4,1,1,2048]{3,2,1,0:T(1,128)S(1)}, f32[4,1,1,2048]{3,2,1,0:T(1,128)S(1)}, u32[]{:S(2)}, u32[]{:S(2)}) collective-permute-start(f32[4,1,1,2048]{3,2,1,0:T(1,128)S(1)} %get-tuple-element.12), channel_id=1, source_target_pairs={{0,1},{1,2},{2,3},{3,4},{4,5},{5,6},{6,7},{7,8},{8,9},{9,10},{10,1... | collective-permute-start | bytes 98312 | tf_op jit(solution)/shard_map/ppermute | solution.py:18
  11.4 2.7 %convert_element_type.63 = bf16[4,1,64,2048]{3,2,1,0:T(8,128)(2,1)} convert(f32[4,1,64,2048]{3,2,1,0:T(8,128)} %param.7) | non-fusion elementwise | flops 524288 | bytes 3145728 | tf_op jit(solution)/shard_map/convert_element_type | solution.py:107
  14.2 0.0 copy-done.3
  14.2 0.0 copy-done.4
  14.2 0.0 copy-start.5
  14.2 0.0 copy-start.6
  14.2 0.0 copy-start
  14.3 12.0 %fusion.25 = f32[256,2048]{1,0:T(8,128)} fusion(bf16[2048,2048]{1,0:T(8,128)(2,1)} %param.9, bf16[256,2048]{1,0:T(8,128)(2,1)} %bitcast.37, f32[2048]{0:T(1024)S(1)} %copy-done.4), kind=kOutput, calls=%fused_computation.38 | convolution fusion | flops 4296015872 | bytes 11542528 | tf_op jit(solution)/shard_map/dot_general | solution.py:45
  26.3 0.0 copy-done.5
  26.3 0.0 copy-done.6
  26.3 0.2 select_reduce_fusion
  26.5 0.0 collective-permute-done
  26.6 0.0 collective-permute-done.1
  26.6 1.8 collective-permute-done.2
  28.3 0.0 copy-done
  28.3 3.5 %fusion.15 = bf16[4,1,64,2048]{3,2,1,0:T(8,128)(2,1)S(1)} fusion(f32[4,1,64,2048]{3,2,1,0:T(8,128)} %param.8, f32[4,1,64,2048]{3,2,1,0:T(8,128)} %collective-permute-done.2, f32[4,1,64,2048]{3,2,1,0:T(8,128)S(1)} %copy-done, f32[4,1,1,2048]{3,2,1,0:T(1,128)S(1)} %collective-permute-done.1, f32[4,1,1,2048]{3,2,1,0:T(1,128)S(1)} %collective-permute-done, ...), kind=kLoop, calls=%fused_computation.21 | loop fusion | flops 8912896 | bytes 10027028 | tf_op jit(solution)/shard_map/convert_element_type | solution.py:117
  31.9 1.8 copy.66
  33.7 10.6 %all-to-all-start = ((bf16[4,1,64,2048]{3,0,1,2:T(4,128)(2,1)}), bf16[4,1,64,2048]{3,0,1,2:T(4,128)(2,1)S(1)}, u32[]{:S(2)}, u32[]{:S(2)}) async-start(bf16[4,1,64,2048]{3,0,1,2:T(4,128)(2,1)} %copy.66), calls=%async_computation | async-start | bytes 2097152 | tf_op jit(solution)/shard_map/all_to_all | solution.py:118
  44.5 0.1 broadcast_subtract_fusion
  44.6 1.2 broadcast_add_fusion
  45.7 26.6 %all-to-all-done = bf16[4,1,64,2048]{3,0,1,2:T(4,128)(2,1)S(1)} async-done(((bf16[4,1,64,2048]{3,0,1,2:T(4,128)(2,1)}), bf16[4,1,64,2048]{3,0,1,2:T(4,128)(2,1)S(1)}, u32[]{:S(2)}, u32[]{:S(2)}) %all-to-all-start) | async-done | bytes 1048608 | tf_op jit(solution)/shard_map/all_to_all | solution.py:118
  72.3 1.6 fusion.4
  73.9 1.6 fusion.5
  75.6 0.2 pad_maximum_fusion.2
  75.8 3.0 %copy.69 = bf16[8,16,4,2048]{3,2,1,0:T(4,128)(2,1)} copy(bf16[8,16,4,2048]{3,1,2,0:T(8,128)(2,1)S(1)} %pad_maximum_fusion.2) | data formatting | bytes 4194304 | tf_op jit(solution)/shard_map/concatenate | solution.py:56
  78.7 4.0 %convert_element_type.68 = bf16[512,2048]{1,0:T(8,128)(2,1)} reshape(bf16[8,16,4,2048]{3,2,1,0:T(4,128)(2,1)} %copy.69) | data formatting | bytes 4194304 | tf_op jit(solution)/shard_map/convert_element_type | solution.py:56
  82.7 7.6 %fusion.62 = f32[512,2048]{1,0:T(8,128)S(1)} fusion(bf16[512,2048]{1,0:T(8,128)(2,1)} %convert_element_type.68, bf16[2048,2048]{1,0:T(8,128)(2,1)} %param.9), kind=kOutput, calls=%fused_computation.84 | convolution fusion | flops 4294967296 | bytes 14680064 | tf_op jit(solution)/shard_map/dot_general | solution.py:58
  90.3 2.3 %fusion.59 = (f32[256,2048]{1,0:T(8,128)}, f32[256,2048]{1,0:T(8,128)}) fusion(f32[512,2048]{1,0:T(8,128)S(1)} %fusion.62), kind=kLoop, calls=%fused_computation.81 | loop fusion | bytes 8388608 | tf_op jit(solution)/shard_map/slice | solution.py:67
  92.6 2.9 %squeeze.14 = f32[4,16,4,2048]{3,2,1,0:T(4,128)} reshape(f32[256,2048]{1,0:T(8,128)} %get-tuple-element.8) | data formatting | bytes 4194304 | tf_op jit(solution)/shard_map/squeeze | solution.py:67
  95.4 0.0 copy-start.1
  95.4 0.0 copy-start.2
  95.4 2.9 %squeeze.15 = f32[4,16,4,2048]{3,2,1,0:T(4,128)} reshape(f32[256,2048]{1,0:T(8,128)} %get-tuple-element.7) | data formatting | bytes 4194304 | tf_op jit(solution)/shard_map/squeeze | solution.py:67
  98.4 0.0 copy-done.1
  98.4 0.0 copy-done.2
  98.4 3.3 %fusion.18 = (bf16[4,16,4,2048]{3,2,1,0:T(4,128)(2,1)S(1)}, bf16[4,16,4,2048]{3,2,1,0:T(4,128)(2,1)S(1)}) fusion(f32[4,16,4,2048]{3,2,1,0:T(4,128)} %squeeze.15, f32[4,16,4,2048]{3,2,1,0:T(4,128)} %squeeze.14, f32[4,16,2048]{2,1,0:T(8,128)S(1)} %copy-done.2, f32[16]{0:T(128)S(1)} %sine_multiply_fusion, f32[4,16,2048]{2,1,0:T(8,128)S(1)} %copy-done.1), kind=kLoop, calls=%fused_computation.31 | loop fusion | flops 5242880 | bytes 7340096 | tf_op jit(solution)/shard_map/convert
  101.7 2.7 %pad_maximum_fusion.3 = bf16[8,16,4,2048]{3,2,1,0:T(4,128)(2,1)} fusion(bf16[4,16,4,2048]{3,2,1,0:T(4,128)(2,1)S(1)} %get-tuple-element.6, bf16[4,16,4,2048]{3,2,1,0:T(4,128)(2,1)S(1)} %get-tuple-element.5), kind=kLoop, calls=%fused_computation.26 | loop fusion | flops 1048576 | bytes 4194304 | tf_op jit(solution)/shard_map/concatenate | solution.py:70
  104.4 4.0 %convert_element_type.70 = bf16[512,2048]{1,0:T(8,128)(2,1)} reshape(bf16[8,16,4,2048]{3,2,1,0:T(4,128)(2,1)} %pad_maximum_fusion.3) | data formatting | bytes 4194304 | tf_op jit(solution)/shard_map/convert_element_type | solution.py:71
  108.3 8.5 %convolution_convert_fusion = bf16[512,2048]{1,0:T(8,128)(2,1)S(1)} fusion(bf16[512,2048]{1,0:T(8,128)(2,1)} %convert_element_type.70, bf16[2048,2048]{1,0:T(8,128)(2,1)} %param.9), kind=kOutput, calls=%fused_computation | convolution fusion | flops 4296015872 | bytes 12582912 | tf_op jit(solution)/shard_map/dot_general | solution.py:45
  116.9 1.5 fusion.60
  118.3 1.5 squeeze.16
  119.8 2.7 %fusion.21 = f32[4,4,2048,16]{2,3,1,0:T(8,128)} fusion(bf16[4,16,4,2048]{3,2,1,0:T(4,128)(2,1)S(1)} %squeeze.16), kind=kOutput, calls=%fused_computation.34 | convolution fusion | flops 100666880 | bytes 3145728 | tf_op jit(solution)/shard_map/kn,fnrx->fkrx/dot_general | solution.py:39
  122.5 1.5 squeeze.17
  123.9 3.1 %fusion.1 = f32[4,16,4,2048]{3,1,2,0:T(8,128)S(1)} fusion(f32[4,4,2048,16]{2,3,1,0:T(8,128)} %fusion.21, bf16[4,16,4,2048]{3,2,1,0:T(4,128)(2,1)S(1)} %squeeze.17), kind=kOutput, calls=%fused_computation.5 | convolution fusion | flops 101715456 | bytes 5242880 | tf_op jit(solution)/shard_map/kn,fnrx->fkrx/dot_general | solution.py:39
  127.0 2.7 %copy.72 = f32[4,16,4,2048]{3,2,0,1:T(4,128)} copy(f32[4,16,4,2048]{3,1,2,0:T(8,128)S(1)} %fusion.1) | data formatting | bytes 4194304 | tf_op jit(solution)/shard_map/div | solution.py:126
  129.7 4.6 %all-to-all-start.1 = ((f32[4,16,4,2048]{3,2,0,1:T(4,128)}), f32[4,16,4,2048]{3,2,0,1:T(4,128)}, u32[]{:S(2)}, u32[]{:S(2)}) async-start(f32[4,16,4,2048]{3,2,0,1:T(4,128)} %copy.72), calls=%async_computation.1 | async-start | bytes 4194304 | tf_op jit(solution)/shard_map/all_to_all | solution.py:129
  134.3 47.9 %all-to-all-done.1 = f32[4,16,4,2048]{3,2,0,1:T(4,128)} async-done(((f32[4,16,4,2048]{3,2,0,1:T(4,128)}), f32[4,16,4,2048]{3,2,0,1:T(4,128)}, u32[]{:S(2)}, u32[]{:S(2)}) %all-to-all-start.1) | async-done | bytes 2097184 | tf_op jit(solution)/shard_map/all_to_all | solution.py:129
  182.2 2.8 %copy_multiply_fusion = f32[4,16,4,2048]{3,1,2,0:T(8,128)S(1)} fusion(f32[4,16,4,2048]{3,2,0,1:T(4,128)} %all-to-all-done.1, f32[]{:T(128)S(6)} %pow.8), kind=kLoop, calls=%fused_computation.28 | loop fusion | flops 524288 | bytes 4194308 | tf_op jit(solution)/shard_map/mul | solution.py:130
  185.0 1.4 copy.74
  186.4 2.6 %copy_add_fusion = f32[4,1,64,2048]{3,2,1,0:T(8,128)} fusion(f32[4,1,64,2048]{3,2,1,0:T(8,128)S(1)} %copy-done, f32[4,1,64,2048]{3,0,2,1:T(4,128)S(1)} %bitcast.35), kind=kLoop, calls=%fused_computation.27 | loop fusion | flops 524288 | bytes 6291456 | tf_op jit(solution)/shard_map/add | solution.py:130
  (5 shorter events, 0.2 us)
Async XLA Ops:
  0.0 14.2 %copy-start.3 = (s32[64,2048]{1,0:T(8,128)S(1)}, s32[64,2048]{1,0:T(8,128)}, u32[]{:S(2)}) copy-start(s32[64,2048]{1,0:T(8,128)} %param.13) | copy-start | bytes 1572868
  0.0 28.3 %collective-permute-start.2 = (f32[4,1,64,2048]{3,2,1,0:T(8,128)}, f32[4,1,64,2048]{3,2,1,0:T(8,128)}, u32[]{:S(2)}, u32[]{:S(2)}) collective-permute-start(f32[4,1,64,2048]{3,2,1,0:T(8,128)} %param.7), channel_id=1, source_target_pairs={{0,16},{16,32},{32,48},{48,64},{64,80},{80,96},{96,112},{112,128},... | collective-permute-start | bytes 6291464 | tf_op jit(solution)/shard_map/ppermute | solution.py:29
  6.1 20.4 %collective-permute-start = (f32[4,1,1,2048]{3,2,1,0:T(1,128)S(1)}, f32[4,1,1,2048]{3,2,1,0:T(1,128)S(1)}, u32[]{:S(2)}, u32[]{:S(2)}) collective-permute-start(f32[4,1,1,2048]{3,2,1,0:T(1,128)S(1)} %get-tuple-element.11), channel_id=1, source_target_pairs={{1,0},{2,1},{3,2},{4,3},{5,4},{6,5},{7,6},{8,7},{9,8},{10,9},{11,1... | collective-permute-start | bytes 98312 | tf_op jit(solution)/shard_map/ppermute | solution.py:21
  7.4 6.8 %copy-start.4 = (f32[2048]{0:T(1024)S(1)}, f32[2048]{0:T(1024)}, u32[]{:S(2)}) copy-start(f32[2048]{0:T(1024)} %param.10) | copy-start | bytes 24580
  7.5 19.1 %collective-permute-start.1 = (f32[4,1,1,2048]{3,2,1,0:T(1,128)S(1)}, f32[4,1,1,2048]{3,2,1,0:T(1,128)S(1)}, u32[]{:S(2)}, u32[]{:S(2)}) collective-permute-start(f32[4,1,1,2048]{3,2,1,0:T(1,128)S(1)} %get-tuple-element.12), channel_id=1, source_target_pairs={{0,1},{1,2},{2,3},{3,4},{4,5},{5,6},{6,7},{7,8},{8,9},{9,10},{10,1... | collective-permute-start | bytes 98312 | tf_op jit(solution)/shard_map/ppermute | solution.py:18
  14.2 12.1 %copy-start.5 = (f32[8]{0:T(128)S(1)}, f32[8]{0:T(128)}, u32[]{:S(2)}) copy-start(f32[8]{0:T(128)} %param.11) | copy-start | bytes 100
  14.2 12.1 %copy-start.6 = (s32[4]{0:T(128)S(1)}, s32[4]{0:T(128)}, u32[]{:S(2)}) copy-start(s32[4]{0:T(128)} %param.12) | copy-start | bytes 52
  14.2 14.1 %copy-start = (f32[4,1,64,2048]{3,2,1,0:T(8,128)S(1)}, f32[4,1,64,2048]{3,2,1,0:T(8,128)}, u32[]{:S(2)}) copy-start(f32[4,1,64,2048]{3,2,1,0:T(8,128)} %param.7) | copy-start | bytes 6291460
  33.7 38.6 %all-to-all-start = ((bf16[4,1,64,2048]{3,0,1,2:T(4,128)(2,1)}), bf16[4,1,64,2048]{3,0,1,2:T(4,128)(2,1)S(1)}, u32[]{:S(2)}, u32[]{:S(2)}) async-start(bf16[4,1,64,2048]{3,0,1,2:T(4,128)(2,1)} %copy.66), calls=%async_computation | async-start | bytes 2097152 | tf_op jit(solution)/shard_map/all_to_all | solution.py:118
  95.4 3.0 %copy-start.1 = (f32[4,16,2048]{2,1,0:T(8,128)S(1)}, f32[4,16,2048]{2,1,0:T(8,128)}, u32[]{:S(2)}) copy-start(f32[4,16,2048]{2,1,0:T(8,128)} %get-tuple-element.13) | copy-start | bytes 1572868
  95.4 3.0 %copy-start.2 = (f32[4,16,2048]{2,1,0:T(8,128)S(1)}, f32[4,16,2048]{2,1,0:T(8,128)}, u32[]{:S(2)}) copy-start(f32[4,16,2048]{2,1,0:T(8,128)} %get-tuple-element.14) | copy-start | bytes 1572868
  129.7 52.5 %all-to-all-start.1 = ((f32[4,16,4,2048]{3,2,0,1:T(4,128)}), f32[4,16,4,2048]{3,2,0,1:T(4,128)}, u32[]{:S(2)}, u32[]{:S(2)}) async-start(f32[4,16,4,2048]{3,2,0,1:T(4,128)} %copy.72), calls=%async_computation.1 | async-start | bytes 4194304 | tf_op jit(solution)/shard_map/all_to_all | solution.py:129
where the time goes:
time: 190 us; the launch traced here: 189 us
  waiting for transfers between devices  76.3 us (40%)
  matrix products  37.2 us (20%)
  local copies, waits for them, and re-layouts  30.3 us (16%)
  starting transfers between devices  25.6 us (13%)
  other arithmetic  19.5 us (10%)
    all_to_all x1, waiting for transfers between devices, on_device(): lax.all_to_all(relaxed_rows, 'tm', split_axis=1, concat_axis=2, tiled=True)  47.9 us
    all_to_all x1, waiting for transfers between devices, on_device(): lax.all_to_all(scaled, 'tm', split_axis=2, concat_axis=1, tiled=True)  26.6 us
    dot_general x2, matrix products, to_space(): lax.dot_general(modal, eigenbasis, (((1,), (1,)), ((), ())), preferred_el...  20.6 us
    all_to_all x1, starting transfers between devices, on_device(): lax.all_to_all(scaled, 'tm', split_axis=2, concat_axis=1, tiled=True)  10.6 us
    dot_general x4, matrix products, apply_table(): jnp.einsum('kn,fnrx->fkrx', table, values.astype(jnp.float32), precision=...  9.01 us
    dot_general x1, matrix products, solve_shifted(): jnp.dot(stacked, eigenbasis, preferred_element_type=jnp.float32)  7.56 us
    squeeze x2, local copies, waits for them, and re-layouts, solve_shifted(): scaled_real = (modal[0] * shift_real + modal[1] * shift_imag) / magnitude  5.81 us
    ppermute x1, starting transfers between devices, from_behind(): lax.ppermute(value, axis, [(source, source + steps) for source in range(i...  5.05 us
  transfers between devices with their start and end apart: 5, of which 3 were waited for; matrix products, arithmetic and copies ran while one was open for 9% of the time, Pallas kernels for 0%

commit v1 on v0

v1 whole, which is shorter than its diff:
```python
import functools

import jax
import jax.numpy as jnp
from jax import lax
from jax.experimental import pallas as pl
from jax.experimental.pallas import tpu as pltpu
from jax.sharding import PartitionSpec as P

ALPHA = 0.5
DIFF = 0.06
DEPO = 0.1
MESH = pl.DeviceIdType.MESH
CHIPS = 8
F32, BF16 = jnp.float32, jnp.bfloat16


def nt(a, b):
    return lax.dot_general(a, b, (((1,), (1,)), ((), ())), preferred_element_type=F32)


def nn(a, b):
    return jnp.dot(a, b, preferred_element_type=F32)


def kernel(
    F, R, X, SP,
    table_s, class_s, c_h, f_h, e_h, lam_h, bed_h, out_h,
    c_v, f_v, e_v, lam_v, bed_v, cb_v, q_v, cp_v, rb_v, edge_v, halo_v, dinv_v, dp_v, cl_v,
    a_v, ar_v, p0_v, p1_v, cs_v, cr_v, bs_v, bf_v, bb_v, zs_v, wz_v, acc_v,
    ld, e_sem, h_ss, h_rs, a_ss, a_rs, c_ss, c_rs, bo_ss, bf_ss, bf_rs, bb_ss, bb_rs, z_ss, z_rs, o_sem,
):
    TN = X // CHIPS
    H = F // 2
    t = lax.axis_index("tm")
    sp = lax.axis_index("space")
    z, h = t // 2, t % 2
    partner = (z * 2 + 1 - h, sp)
    nxt = (((z + 1) % CHIPS) * 2 + h, sp)
    prv = (((z + CHIPS - 1) % CHIPS) * 2 + h, sp)
    below = (t, (sp + 1) % SP)
    above = (t, (sp + SP - 1) % SP)

    def cols(j):
        return pl.ds(pl.multiple_of(j * TN, TN), TN)

    def load_e(j):
        return pltpu.make_async_copy(e_h.at[:, cols(j)], e_v.at[:, cols(j)], e_sem.at[j])

    ld_c = pltpu.make_async_copy(c_h, c_v, ld.at[0])
    ld_l = pltpu.make_async_copy(lam_h, lam_v, ld.at[1])
    ld_f = pltpu.make_async_copy(f_h, f_v, ld.at[2])
    ld_b = pltpu.make_async_copy(bed_h, bed_v, ld.at[3])
    ld_c.start()
    ld_l.start()
    for j in range(CHIPS):
        load_e(j).start()
    ld_f.start()
    ld_b.start()

    barrier = pltpu.get_barrier_semaphore()
    for dev in (partner, nxt, prv, below, above):
        pl.semaphore_signal(barrier, inc=1, device_id=dev, device_id_type=MESH)

    ld_l.wait()
    settling = [table_s[class_s[f]] for f in range(F)]
    for j in range(CHIPS):
        for f in range(F):
            dinv_v[f, j] = 1.0 / (1.0 + 2.0 * DIFF + settling[f] - lam_v[:, j * TN:(j + 1) * TN])

    for i in range(H):
        base = dinv_v[H * h + i]
        power = base
        dp_v[1, i] = power
        for m in range(2, 2 * CHIPS + 1):
            power = power * base
            dp_v[m, i] = power
        cl_v[i] = 1.0 / (1.0 - ALPHA * power)

    ld_c.wait()
    cb_v[...] = c_v[...].astype(BF16)
    for f in range(F):
        edge_v[0, f:f + 1, :] = c_v[(f + 1) * R - 1:(f + 1) * R, :]
        edge_v[1, f:f + 1, :] = c_v[f * R:f * R + 1, :]

    def first(j, carry):
        load_e(j).wait()
        q = nn(cb_v[...], e_v[:, cols(j)])
        q_v[j] = q
        cp_v[:, cols(j)] = (q * lam_v[:, cols(j)]).astype(BF16)
        return carry

    lax.fori_loop(0, CHIPS, first, 0)

    pl.semaphore_wait(barrier, 5)

    def halo(i, dev):
        return pltpu.make_async_remote_copy(
            edge_v.at[i], halo_v.at[i], h_ss.at[i], h_rs.at[i], device_id=dev, device_id_type=MESH
        )

    halo(0, below).start()
    halo(1, above).start()
    ld_f.wait()
    ld_b.wait()

    row = lax.broadcasted_iota(jnp.int32, (R, TN), 0)
    has_above = jnp.where(sp > 0, 1.0, 0.0).astype(F32)
    has_below = jnp.where(sp < SP - 1, 1.0, 0.0).astype(F32)

    halo(0, below).wait()
    halo(1, above).wait()

    def second(j, carry):
        along = nt(cp_v[...], e_v[cols(j), :])
        bed = DEPO * bed_v[:, cols(j)].astype(F32)
        for f in range(F):
            rows = slice(f * R, (f + 1) * R)
            c = c_v[rows, cols(j)]
            up = jnp.where(row == 0, halo_v[0, f:f + 1, cols(j)] * has_above, pltpu.roll(c, 1, 0))
            low = jnp.where(row == R - 1, halo_v[1, f:f + 1, cols(j)] * has_below, pltpu.roll(c, R - 1, 0))
            vert = DIFF * (low - 2.0 * c + up) + settling[f] * (up - c) - bed * c
            rest = f_v[rows, cols(j)] - (c - cb_v[rows, cols(j)].astype(F32)) + along[rows] + vert
            rb_v[rows, cols(j)] = rest.astype(BF16)
        return carry

    lax.fori_loop(0, CHIPS, second, 0)

    keep = jnp.where(t < 2 * CHIPS - 1, 1.0, 0.0).astype(F32)
    sigma = jnp.where(z == 0, ALPHA, 1.0).astype(F32)

    def chunk(s):
        return (z + CHIPS - s) % CHIPS

    def swap_a(k):
        return pltpu.make_async_remote_copy(
            a_v.at[k, pl.ds(H * (1 - h), H)], ar_v.at[k], a_ss.at[k], a_rs.at[k],
            device_id=partner, device_id_type=MESH,
        )

    def third(s):
        k = chunk(s)
        m = nn(rb_v[...], e_v[:, cols(k)])
        for f in range(F):
            rows = slice(f * R, (f + 1) * R)
            q = q_v[k, rows, :]
            a_v[k, f] = (m[rows] - q) * dinv_v[f, k] + keep * q
        swap_a(k).start()

    def chain(s, i):
        return pltpu.make_async_remote_copy(
            cs_v.at[s, i], cr_v.at[s, i], c_ss.at[s, i], c_rs.at[s, i],
            device_id=nxt, device_id_type=MESH,
        )

    def own_fwd(i):
        return pltpu.make_async_remote_copy(
            bs_v.at[i], bf_v.at[0, i], bo_ss.at[0, i], bf_rs.at[0, i],
            device_id=nxt, device_id_type=MESH,
        )

    def own_bwd(i):
        return pltpu.make_async_remote_copy(
            bs_v.at[i], bb_v.at[0, i], bo_ss.at[1, i], bb_rs.at[0, i],
            device_id=prv, device_id_type=MESH,
        )

    def relay_fwd(j, i):
        return pltpu.make_async_remote_copy(
            bf_v.at[j, i], bf_v.at[j + 1, i], bf_ss.at[j, i], bf_rs.at[j + 1, i],
            device_id=nxt, device_id_type=MESH,
        )

    def relay_bwd(j, i):
        return pltpu.make_async_remote_copy(
            bb_v.at[j, i], bb_v.at[j + 1, i], bb_ss.at[j, i], bb_rs.at[j + 1, i],
            device_id=prv, device_id_type=MESH,
        )

    def local(s, has_input):
        k = chunk(s)
        swap_a(k).wait_recv()
        for i in range(H):
            own, other = a_v[k, H * h + i], ar_v[k, i]
            a0 = jnp.where(h == 0, own, other)
            a1 = jnp.where(h == 0, other, own)
            d = dp_v[1, i, k]
            if has_input:
                chain(s - 1, i).wait_recv()
                a0 = a0 + (sigma * d) * cr_v[s - 1, i].astype(F32)
            p1 = a1 + d * a0
            p0_v[k, i] = a0
            p1_v[k, i] = p1
            yield i, p1

    third(0)
    third(1)
    for i, p1 in local(0, False):
        cs_v[0, i] = p1.astype(BF16)
        chain(0, i).start()

    def middle(s, carry):
        third(s + 1)
        for i, p1 in local(s, True):
            cs_v[s, i] = p1.astype(BF16)
            chain(s, i).start()
        return carry

    lax.fori_loop(1, CHIPS - 1, middle, 0)

    def swap_z(k, i):
        return pltpu.make_async_remote_copy(
            zs_v.at[k, i], wz_v.at[k, H * h + i], z_ss.at[k, i], z_rs.at[k, i],
            device_id=partner, device_id_type=MESH,
        )

    def stage(s, i, ze):
        k = chunk(s)
        wrap = jnp.where(s >= z, ALPHA, 1.0).astype(F32)
        ze = ze * wrap
        z0 = p0_v[k, i] + dp_v[2 * s + 1, i, k] * ze
        z1 = p1_v[k, i] + dp_v[2 * s + 2, i, k] * ze
        zs_v[k, i] = jnp.where(h == 0, z1, z0)
        swap_z(k, i).start()
        wz_v[k, H * h + i] = jnp.where(h == 0, z0, z1)

    def finish(s, base):
        k = chunk(s)
        for i in range(H):
            swap_z(k, i).wait_recv()
        w = jnp.concatenate(
            [wz_v[k, f] - keep * q_v[k, f * R:(f + 1) * R, :] for f in range(F)], axis=0
        ).astype(BF16)
        step = 2 * TN

        def part(n, carry):
            cs = pl.ds(pl.multiple_of(n * step, step), step)
            acc_v[:, cs] = base[:, cs] + nt(w, e_v[cs, cols(k)])
            return carry

        lax.fori_loop(0, X // step, part, 0)

    last = CHIPS - 1
    for i, p1 in local(last, True):
        ze = p1 * cl_v[i, chunk(last)]
        bs_v[i] = ze.astype(BF16)
        own_fwd(i).start()
        own_bwd(i).start()
        stage(last, i, ze)

    def got_fwd(j, relay):
        for i in range(H):
            (own_fwd(i) if j == 0 else relay_fwd(j - 1, i)).wait_recv()
            if relay:
                relay_fwd(j, i).start()
        for i in range(H):
            stage(j, i, bf_v[j, i].astype(F32))

    def got_bwd(j, relay):
        for i in range(H):
            (own_bwd(i) if j == 0 else relay_bwd(j - 1, i)).wait_recv()
            if relay:
                relay_bwd(j, i).start()
        for i in range(H):
            stage(CHIPS - 2 - j, i, bb_v[j, i].astype(F32))

    got_fwd(0, True)
    got_bwd(0, True)
    finish(last, c_v)
    got_fwd(1, True)
    got_bwd(1, True)
    finish(0, acc_v)
    finish(CHIPS - 2, acc_v)
    got_fwd(2, True)
    got_bwd(2, False)
    finish(1, acc_v)
    finish(CHIPS - 3, acc_v)
    got_fwd(3, False)
    finish(2, acc_v)
    finish(CHIPS - 4, acc_v)
    finish(3, acc_v)

    store = pltpu.make_async_copy(acc_v, out_h, o_sem)
    store.start()

    for k in range(CHIPS):
        swap_a(k).wait_send()
        for i in range(H):
            swap_z(k, i).wait_send()
    for i in range(H):
        for s in range(CHIPS - 1):
            chain(s, i).wait_send()
        own_fwd(i).wait_send()
        own_bwd(i).wait_send()
        for j in range(3):
            relay_fwd(j, i).wait_send()
        for j in range(2):
            relay_bwd(j, i).wait_send()
    store.wait()


def on_device(c, f, e, lam, table, cls, bed):
    F, S, R, X = c.shape
    SP = lax.axis_size("space")
    TN, H, M = X // CHIPS, F // 2, F * R
    any_spec = pl.BlockSpec(memory_space=pl.ANY)
    smem_spec = pl.BlockSpec(memory_space=pltpu.SMEM)
    dma = pltpu.SemaphoreType.DMA
    out = pl.pallas_call(
        functools.partial(kernel, F, R, X, SP),
        out_shape=jax.ShapeDtypeStruct((M, X), F32),
        in_specs=[smem_spec, smem_spec] + [any_spec] * 5,
        out_specs=any_spec,
        scratch_shapes=[
            pltpu.VMEM((M, X), F32),
            pltpu.VMEM((M, X), F32),
            pltpu.VMEM((X, X), BF16),
            pltpu.VMEM((1, X), F32),
            pltpu.VMEM((R, X), jnp.int32),
            pltpu.VMEM((M, X), BF16),
            pltpu.VMEM((CHIPS, M, TN), F32),
            pltpu.VMEM((M, X), BF16),
            pltpu.VMEM((M, X), BF16),
            pltpu.VMEM((2, F, X), F32),
            pltpu.VMEM((2, F, X), F32),
            pltpu.VMEM((F, CHIPS, 1, TN), F32),
            pltpu.VMEM((2 * CHIPS + 1, H, CHIPS, 1, TN), F32),
            pltpu.VMEM((H, CHIPS, 1, TN), F32),
            pltpu.VMEM((CHIPS, F, R, TN), F32),
            pltpu.VMEM((CHIPS, H, R, TN), F32),
            pltpu.VMEM((CHIPS, H, R, TN), F32),
            pltpu.VMEM((CHIPS, H, R, TN), F32),
            pltpu.VMEM((CHIPS - 1, H, R, TN), BF16),
            pltpu.VMEM((CHIPS - 1, H, R, TN), BF16),
            pltpu.VMEM((H, R, TN), BF16),
            pltpu.VMEM((4, H, R, TN), BF16),
            pltpu.VMEM((3, H, R, TN), BF16),
            pltpu.VMEM((CHIPS, H, R, TN), F32),
            pltpu.VMEM((CHIPS, F, R, TN), F32),
            pltpu.VMEM((M, X), F32),
            dma((4,)),
            dma((CHIPS,)),
            dma((2,)), dma((2,)),
            dma((CHIPS,)), dma((CHIPS,)),
            dma((CHIPS - 1, H)), dma((CHIPS - 1, H)),
            dma((2, H)),
            dma((3, H)), dma((4, H)),
            dma((2, H)), dma((3, H)),
            dma((CHIPS, H)), dma((CHIPS, H)),
            dma,
        ],
        compiler_params=pltpu.CompilerParams(
            collective_id=0, has_side_effects=True, vmem_limit_bytes=60 * 1024 * 1024
        ),
    )(
        table, cls, c.reshape(M, X), f.reshape(M, X), e, lam.reshape(1, X), bed,
    )
    return out.reshape(F, S, R, X)


def solution(mesh):
    return jax.shard_map(
        on_device,
        mesh=mesh,
        in_specs=(
            P(None, "tm", "space", None),
            P(None, "tm", "space", None),
            P(),
            P(),
            P(),
            P(),
            P("space", None),
        ),
        out_specs=P(None, "tm", "space", None),
        check_vma=False,
    )
```

time: 190 us -> 69.6 us (0.37)
  waiting for transfers between devices: 76.3 us -> 0 us
  Pallas kernels: 0 us -> 66.4 us
  matrix products: 37.2 us -> 0 us
  local copies, waits for them, and re-layouts: 30.3 us -> 3.14 us
  starting transfers between devices: 25.6 us -> 0 us
  other arithmetic: 19.5 us -> 0 us
    all_to_all x2 -> x0, waiting for transfers between devices: 74.5 us -> none  [the longest x1 47.9 us: on_device(): lax.all_to_all(relaxed_rows, 'tm', split_axis=1, concat_axis=2, tiled=True)]
    pallas_call x0 -> x1, Pallas kernels: none -> 66.4 us  [on_device(): pl.pallas_call(functools.partial(kernel, F, R, X, SP), out_shape=jax.Shap...]
    dot_general x7 -> x0, matrix products: 37.2 us -> none  [the longest x2 20.6 us: to_space(): lax.dot_general(modal, eigenbasis, (((1,), (1,)), ((), ())), preferred_el...]
    all_to_all x2 -> x0, starting transfers between devices: 15.2 us -> none  [the longest x1 10.6 us: on_device(): lax.all_to_all(scaled, 'tm', split_axis=2, concat_axis=1, tiled=True)]
    ppermute x3 -> x0, starting transfers between devices: 10.3 us -> none  [the longest x1 5.05 us: from_behind(): lax.ppermute(value, axis, [(source, source + steps) for source in range(i...]
    convert_element_type x3 -> x0, local copies, waits for them, and re-layouts: 9.73 us -> none  [the longest x1 3.98 us: solve_shifted(): scaled = jnp.concatenate([scaled_real, scaled_imag], axis=0).astype(jnp.b...]
    squeeze x4 -> x0, local copies, waits for them, and re-layouts: 8.72 us -> none  [the longest x2 5.81 us: solve_shifted(): scaled_real = (modal[0] * shift_real + modal[1] * shift_imag) / magnitude]
    convert_element_type x2 -> x0, other arithmetic: 6.26 us -> none  [the longest x1 3.55 us: on_device(): scaled = (scale_up[None, :, None, None] * residual).astype(jnp.bfloat16)]
  transfers between devices with their start and end apart: 5 -> 0, of which waited for: 3 -> 0; matrix products, arithmetic and copies ran while one was open for 9% -> 0% of each run, Pallas kernels for 0% -> 0%
where the time goes in v1:
time: 69.6 us; the launch traced here: 69.5 us
  Pallas kernels  66.4 us (95%)
  local copies, waits for them, and re-layouts  3.14 us (5%)
    pallas_call x1, Pallas kernels, on_device(): pl.pallas_call(functools.partial(kernel, F, R, X, SP), out_shape=jax.Shap...  66.4 us
    unnamed x1, local copies, waits for them, and re-layouts  3.14 us

profile of v1, /device:TPU:1, one launch (start us, length us, event | category | flops | bytes accessed | tf_op | source)
XLA Modules:
  0.0 69.5 jit_solution(944837347208708556)
XLA Ops:
  0.0 66.4 %shard_map.73 = f32[256,2048]{1,0:T(8,128)} custom-call(f32[8]{0:T(128)} %table_s.1, s32[4]{0:T(128)} %class_s.1, f32[256,2048]{1,0:T(8,128)} %bitcast.7, f32[256,2048]{1,0:T(8,128)} %bitcast.8, bf16[2048,2048]{1,0:T(8,128)(2,1)} %e_h.1, f32[1,2048]{1,0:T(1,128)} %bitcast.9, s32[64,2048]{1,0:T(8,128)} %bed_h.1), custom_call_target="tpu_custom_call" | custom-call | tf_op jit(solution)/shard_map/pallas_call | solution.py:309
  66.4 3.1 %copy.10 = f32[4,1,64,2048]{3,2,1,0:T(8,128)} copy(f32[4,1,64,2048]{3,2,1,0:T(8,128)} %bitcast.6) | data formatting | bytes 4194304

commit v2 on v1

v2 whole, which is shorter than its diff:
```python
import functools

import jax
import jax.numpy as jnp
from jax import lax
from jax.experimental import pallas as pl
from jax.experimental.pallas import tpu as pltpu
from jax.sharding import PartitionSpec as P

ALPHA = 0.5
DIFF = 0.06
DEPO = 0.1
MESH = pl.DeviceIdType.MESH
ORDER = (4, 3, 5, 2, 6, 1, 7, 0)
CHIPS = 8
F32, BF16 = jnp.float32, jnp.bfloat16


def nt(a, b):
    return lax.dot_general(a, b, (((1,), (1,)), ((), ())), preferred_element_type=F32)


def nn(a, b):
    return jnp.dot(a, b, preferred_element_type=F32)


def kernel(
    F, R, X, SP,
    table_s, class_s, c_h, f_h, e_h, lam_h, bed_h, out_h,
    c_v, f_v, e_v, lam_v, bed_v, cb_v, q_v, cp_v, rb_v, edge_v, halo_v, dinv_v,
    a_v, ar_v, xs_v, xr_v, ys_v, yr_v, zs_v, wz_v, acc_v,
    ld, e_sem, h_ss, h_rs, a_ss, a_rs, g_ss, g_rs, s_ss, s_rs, z_ss, z_rs, o_sem,
):
    TN = X // CHIPS
    H = F // 2
    t = lax.axis_index("tm")
    sp = lax.axis_index("space")
    z, h = t // 2, t % 2
    partner = (z * 2 + 1 - h, sp)
    below = (t, (sp + 1) % SP)
    above = (t, (sp + SP - 1) % SP)

    def cols(j):
        return pl.ds(pl.multiple_of(j * TN, TN), TN)

    def load_e(j):
        return pltpu.make_async_copy(e_h.at[:, cols(j)], e_v.at[:, cols(j)], e_sem.at[j])

    ld_c = pltpu.make_async_copy(c_h, c_v, ld.at[0])
    ld_l = pltpu.make_async_copy(lam_h, lam_v, ld.at[1])
    ld_f = pltpu.make_async_copy(f_h, f_v, ld.at[2])
    ld_b = pltpu.make_async_copy(bed_h, bed_v, ld.at[3])
    ld_c.start()
    ld_l.start()
    for j in range(CHIPS):
        load_e(j).start()
    ld_f.start()
    ld_b.start()

    barrier = pltpu.get_barrier_semaphore()
    rest = [(((z + d) % CHIPS) * 2 + h, sp) for d in range(1, CHIPS)]
    for dev in [partner, below, above] + rest:
        pl.semaphore_signal(barrier, inc=1, device_id=dev, device_id_type=MESH)

    ld_l.wait()
    settling = [table_s[class_s[f]] for f in range(F)]
    for j in range(CHIPS):
        for f in range(F):
            dinv_v[f, j] = 1.0 / (1.0 + 2.0 * DIFF + settling[f] - lam_v[:, j * TN:(j + 1) * TN])

    ld_c.wait()
    cb_v[...] = c_v[...].astype(BF16)
    for f in range(F):
        edge_v[0, f:f + 1, :] = c_v[(f + 1) * R - 1:(f + 1) * R, :]
        edge_v[1, f:f + 1, :] = c_v[f * R:f * R + 1, :]

    def first(j, carry):
        load_e(j).wait()
        q = nn(cb_v[...], e_v[:, cols(j)])
        q_v[j] = q
        cp_v[:, cols(j)] = (q * lam_v[:, cols(j)]).astype(BF16)
        return carry

    lax.fori_loop(0, CHIPS, first, 0)

    pl.semaphore_wait(barrier, CHIPS + 2)

    def halo(i, dev):
        return pltpu.make_async_remote_copy(
            edge_v.at[i], halo_v.at[i], h_ss.at[i], h_rs.at[i], device_id=dev, device_id_type=MESH
        )

    halo(0, below).start()
    halo(1, above).start()
    ld_f.wait()
    ld_b.wait()

    row = lax.broadcasted_iota(jnp.int32, (R, TN), 0)
    has_above = jnp.where(sp > 0, 1.0, 0.0).astype(F32)
    has_below = jnp.where(sp < SP - 1, 1.0, 0.0).astype(F32)

    halo(0, below).wait()
    halo(1, above).wait()

    def second(j, carry):
        along = nt(cp_v[...], e_v[cols(j), :])
        bed = DEPO * bed_v[:, cols(j)].astype(F32)
        for f in range(F):
            rows = slice(f * R, (f + 1) * R)
            c = c_v[rows, cols(j)]
            up = jnp.where(row == 0, halo_v[0, f:f + 1, cols(j)] * has_above, pltpu.roll(c, 1, 0))
            low = jnp.where(row == R - 1, halo_v[1, f:f + 1, cols(j)] * has_below, pltpu.roll(c, R - 1, 0))
            vert = DIFF * (low - 2.0 * c + up) + settling[f] * (up - c) - bed * c
            rest = f_v[rows, cols(j)] - (c - cb_v[rows, cols(j)].astype(F32)) + along[rows] + vert
            rb_v[rows, cols(j)] = rest.astype(BF16)
        return carry

    lax.fori_loop(0, CHIPS, second, 0)

    keep = jnp.where(t < 2 * CHIPS - 1, 1.0, 0.0).astype(F32)
    sigma = jnp.where(z == 0, ALPHA, 1.0).astype(F32)

    def swap_a(k):
        return pltpu.make_async_remote_copy(
            a_v.at[k, pl.ds(H * (1 - h), H)], ar_v.at[k], a_ss.at[k], a_rs.at[k],
            device_id=partner, device_id_type=MESH,
        )

    def third(k):
        m = nn(rb_v[...], e_v[:, cols(k)])
        for f in range(F):
            rows = slice(f * R, (f + 1) * R)
            q = q_v[k, rows, :]
            a_v[k, f] = (m[rows] - q) * dinv_v[f, k] + keep * q
        swap_a(k).start()

    def chip(d):
        return (z + d) % CHIPS

    def gather(d, i):
        return pltpu.make_async_remote_copy(
            xs_v.at[d, i], xr_v.at[d, i], g_ss.at[d, i], g_rs.at[d, i],
            device_id=(chip(d) * 2 + h, sp), device_id_type=MESH,
        )

    def give(d, i):
        return pltpu.make_async_remote_copy(
            ys_v.at[d, i], yr_v.at[d, i], s_ss.at[d, i], s_rs.at[d, i],
            device_id=(chip(d) * 2 + h, sp), device_id_type=MESH,
        )

    def pair(k, i):
        own, other = a_v[k, H * h + i], ar_v[k, i]
        return jnp.where(h == 0, own, other), jnp.where(h == 0, other, own)

    def partial(d):
        k = chip(d)
        swap_a(k).wait_recv()
        for i in range(H):
            a0, a1 = pair(k, i)
            xs_v[d, i] = (a1 + dinv_v[H * h + i, k] * a0).astype(BF16)
            if d and i == 0:
                gather(d, 0).start()

    third(chip(ORDER[0]))
    for prev, d in zip(ORDER[:-1], ORDER[1:]):
        third(chip(d))
        partial(prev)
    partial(ORDER[-1])
    for i in range(1, H):
        for d in ORDER[:-1]:
            gather(d, i).start()

    def solve(i):
        d1 = dinv_v[H * h + i, z]
        d2 = d1 * d1
        d4 = d2 * d2
        d8 = d4 * d4
        for d in ORDER[:-1]:
            gather(d, i).wait_recv()
        xr_v[0, i] = xs_v[0, i]

        def part(c):
            return xr_v[(z - c + CHIPS) % CHIPS, i].astype(F32)

        total = part(0)
        for c in range(1, CHIPS):
            total = part(c) + d2 * total
        state = total / (1.0 - ALPHA * (d8 * d8))
        for c in range(CHIPS):
            ys_v[(c - z + CHIPS) % CHIPS, i] = state.astype(BF16)
            state = part(c) + d2 * (state * ALPHA if c == 0 else state)
        for d in ORDER[:-1]:
            give(d, i).start()
        yr_v[0, i] = ys_v[0, i]

    for i in range(H):
        solve(i)

    def swap_z(k, i):
        return pltpu.make_async_remote_copy(
            zs_v.at[k, i], wz_v.at[k, H * h + i], z_ss.at[k, i], z_rs.at[k, i],
            device_id=partner, device_id_type=MESH,
        )

    def stage(d):
        k = (z - d + CHIPS) % CHIPS
        for i in range(H):
            if d:
                give(d, i).wait_recv()
            a0, a1 = pair(k, i)
            d1 = dinv_v[H * h + i, k]
            z0 = a0 + (sigma * d1) * yr_v[d, i].astype(F32)
            z1 = a1 + d1 * z0
            zs_v[k, i] = jnp.where(h == 0, z1, z0)
            swap_z(k, i).start()
            wz_v[k, H * h + i] = jnp.where(h == 0, z0, z1)

    def finish(d, base):
        k = (z - d + CHIPS) % CHIPS
        for i in range(H):
            swap_z(k, i).wait_recv()
        w = jnp.concatenate(
            [wz_v[k, f] - keep * q_v[k, f * R:(f + 1) * R, :] for f in range(F)], axis=0
        ).astype(BF16)
        step = 2 * TN

        def part(n, carry):
            cs = pl.ds(pl.multiple_of(n * step, step), step)
            acc_v[:, cs] = base[:, cs] + nt(w, e_v[cs, cols(k)])
            return carry

        lax.fori_loop(0, X // step, part, 0)

    arrive = (0,) + ORDER[:-1]
    stage(arrive[0])
    for prev, d in zip(arrive[:-1], arrive[1:]):
        stage(d)
        finish(prev, c_v if prev == 0 else acc_v)
    finish(arrive[-1], acc_v)

    store = pltpu.make_async_copy(acc_v, out_h, o_sem)
    store.start()

    for k in range(CHIPS):
        swap_a(k).wait_send()
        for i in range(H):
            swap_z(k, i).wait_send()
    for d in ORDER[:-1]:
        for i in range(H):
            gather(d, i).wait_send()
            give(d, i).wait_send()
    store.wait()


def on_device(c, f, e, lam, table, cls, bed):
    F, S, R, X = c.shape
    SP = lax.axis_size("space")
    TN, H, M = X // CHIPS, F // 2, F * R
    any_spec = pl.BlockSpec(memory_space=pl.ANY)
    smem_spec = pl.BlockSpec(memory_space=pltpu.SMEM)
    dma = pltpu.SemaphoreType.DMA
    out = pl.pallas_call(
        functools.partial(kernel, F, R, X, SP),
        out_shape=jax.ShapeDtypeStruct((M, X), F32),
        in_specs=[smem_spec, smem_spec] + [any_spec] * 5,
        out_specs=any_spec,
        scratch_shapes=[
            pltpu.VMEM((M, X), F32),
            pltpu.VMEM((M, X), F32),
            pltpu.VMEM((X, X), BF16),
            pltpu.VMEM((1, X), F32),
            pltpu.VMEM((R, X), jnp.int32),
            pltpu.VMEM((M, X), BF16),
            pltpu.VMEM((CHIPS, M, TN), F32),
            pltpu.VMEM((M, X), BF16),
            pltpu.VMEM((M, X), BF16),
            pltpu.VMEM((2, F, X), F32),
            pltpu.VMEM((2, F, X), F32),
            pltpu.VMEM((F, CHIPS, 1, TN), F32),
            pltpu.VMEM((CHIPS, F, R, TN), F32),
            pltpu.VMEM((CHIPS, H, R, TN), F32),
            pltpu.VMEM((CHIPS, H, R, TN), BF16),
            pltpu.VMEM((CHIPS, H, R, TN), BF16),
            pltpu.VMEM((CHIPS, H, R, TN), BF16),
            pltpu.VMEM((CHIPS, H, R, TN), BF16),
            pltpu.VMEM((CHIPS, H, R, TN), F32),
            pltpu.VMEM((CHIPS, F, R, TN), F32),
            pltpu.VMEM((M, X), F32),
            dma((4,)),
            dma((CHIPS,)),
            dma((2,)), dma((2,)),
            dma((CHIPS,)), dma((CHIPS,)),
            dma((CHIPS, H)), dma((CHIPS, H)),
            dma((CHIPS, H)), dma((CHIPS, H)),
            dma((CHIPS, H)), dma((CHIPS, H)),
            dma,
        ],
        compiler_params=pltpu.CompilerParams(
            collective_id=0, has_side_effects=True, vmem_limit_bytes=60 * 1024 * 1024
        ),
    )(
        table, cls, c.reshape(M, X), f.reshape(M, X), e, lam.reshape(1, X), bed,
    )
    return out.reshape(F, S, R, X)


def solution(mesh):
    return jax.shard_map(
        on_device,
        mesh=mesh,
        in_specs=(
            P(None, "tm", "space", None),
            P(None, "tm", "space", None),
            P(),
            P(),
            P(),
            P(),
            P("space", None),
        ),
        out_specs=P(None, "tm", "space", None),
        check_vma=False,
    )
```

time: 69.6 us -> 65.5 us (0.941)
  Pallas kernels: 66.4 us -> 62.3 us
    pallas_call x1, Pallas kernels: 66.4 us -> 62.3 us  [on_device(): pl.pallas_call(functools.partial(kernel, F, R, X, SP), out_shape=jax.Shap...]
where the time goes in v2:
time: 65.5 us; the launch traced here: 65.4 us
  Pallas kernels  62.3 us (95%)
  local copies, waits for them, and re-layouts  3.14 us (5%)
    pallas_call x1, Pallas kernels, on_device(): pl.pallas_call(functools.partial(kernel, F, R, X, SP), out_shape=jax.Shap...  62.3 us
    unnamed x1, local copies, waits for them, and re-layouts  3.14 us

profile of v2, /device:TPU:1, one launch (start us, length us, event | category | flops | bytes accessed | tf_op | source)
XLA Modules:
  0.0 65.4 jit_solution(208884009854823408)
XLA Ops:
  0.0 62.3 %shard_map.73 = f32[256,2048]{1,0:T(8,128)} custom-call(f32[8]{0:T(128)} %table_s.1, s32[4]{0:T(128)} %class_s.1, f32[256,2048]{1,0:T(8,128)} %bitcast.7, f32[256,2048]{1,0:T(8,128)} %bitcast.8, bf16[2048,2048]{1,0:T(8,128)(2,1)} %e_h.1, f32[1,2048]{1,0:T(1,128)} %bitcast.9, s32[64,2048]{1,0:T(8,128)} %bed_h.1), custom_call_target="tpu_custom_call" | custom-call | tf_op jit(solution)/shard_map/pallas_call | solution.py:263
  62.3 3.1 %copy.10 = f32[4,1,64,2048]{3,2,1,0:T(8,128)} copy(f32[4,1,64,2048]{3,2,1,0:T(8,128)} %bitcast.6) | data formatting | bytes 4194304

commit v3 on v2

--- a/solution.py
+++ b/solution.py
@@ -13,6 +13,9 @@
 MESH = pl.DeviceIdType.MESH
 ORDER = (4, 3, 5, 2, 6, 1, 7, 0)
 CHIPS = 8
+EB = 16
+EARLY = 2
+AHEAD = 2
 F32, BF16 = jnp.float32, jnp.bfloat16
 
 
@@ -26,10 +29,10 @@
 
 def kernel(
     F, R, X, SP,
-    table_s, class_s, c_h, f_h, e_h, lam_h, bed_h, out_h,
-    c_v, f_v, e_v, lam_v, bed_v, cb_v, q_v, cp_v, rb_v, edge_v, halo_v, dinv_v,
-    a_v, ar_v, xs_v, xr_v, ys_v, yr_v, zs_v, wz_v, acc_v,
-    ld, e_sem, h_ss, h_rs, a_ss, a_rs, g_ss, g_rs, s_ss, s_rs, z_ss, z_rs, o_sem,
+    table_s, class_s, c_h, f_h, e_h, lam_h, bed_h, acc_v,
+    c_v, f_v, e_v, lam_v, bed_v, cb_v, q_v, cp_v, rb_v, edge_v, halo_v, er_v, dinv_v,
+    a_v, ar_v, xs_v, xr_v, ys_v, yr_v, zs_v, wz_v,
+    ld, e_sem, h_ss, h_rs, a_ss, a_rs, g_ss, g_rs, s_ss, s_rs, z_ss, z_rs,
 ):
     TN = X // CHIPS
     H = F // 2
@@ -81,26 +84,20 @@
         cp_v[:, cols(j)] = (q * lam_v[:, cols(j)]).astype(BF16)
         return carry
 
-    lax.fori_loop(0, CHIPS, first, 0)
-
+    def halo(i, dev):
+        return pltpu.make_async_remote_copy(
+            edge_v.at[i], halo_v.at[i], h_ss.at[i], h_rs.at[i], device_id=dev, device_id_type=MESH
+        )
+
+    lax.fori_loop(0, EARLY, first, 0)
     pl.semaphore_wait(barrier, CHIPS + 2)
-
-    def halo(i, dev):
-        return pltpu.make_async_remote_copy(
-            edge_v.at[i], halo_v.at[i], h_ss.at[i], h_rs.at[i], device_id=dev, device_id_type=MESH
-        )
-
     halo(0, below).start()
     halo(1, above).start()
+    lax.fori_loop(EARLY, CHIPS, first, 0)
     ld_f.wait()
     ld_b.wait()
 
     row = lax.broadcasted_iota(jnp.int32, (R, TN), 0)
-    has_above = jnp.where(sp > 0, 1.0, 0.0).astype(F32)
-    has_below = jnp.where(sp < SP - 1, 1.0, 0.0).astype(F32)
-
-    halo(0, below).wait()
-    halo(1, above).wait()
 
     def second(j, carry):
         along = nt(cp_v[...], e_v[cols(j), :])
@@ -108,14 +105,29 @@
         for f in range(F):
             rows = slice(f * R, (f + 1) * R)
             c = c_v[rows, cols(j)]
-            up = jnp.where(row == 0, halo_v[0, f:f + 1, cols(j)] * has_above, pltpu.roll(c, 1, 0))
-            low = jnp.where(row == R - 1, halo_v[1, f:f + 1, cols(j)] * has_below, pltpu.roll(c, R - 1, 0))
+            up = jnp.where(row == 0, 0.0, pltpu.roll(c, 1, 0))
+            low = jnp.where(row == R - 1, 0.0, pltpu.roll(c, R - 1, 0))
             vert = DIFF * (low - 2.0 * c + up) + settling[f] * (up - c) - bed * c
             rest = f_v[rows, cols(j)] - (c - cb_v[rows, cols(j)].astype(F32)) + along[rows] + vert
             rb_v[rows, cols(j)] = rest.astype(BF16)
+            er_v[0, f, :, cols(j)] = rest[:EB]
+            er_v[1, f, :, cols(j)] = rest[R - EB:]
         return carry
 
     lax.fori_loop(0, CHIPS, second, 0)
+
+    halo(0, below).wait()
+    halo(1, above).wait()
+    has_above = jnp.where(sp > 0, 1.0, 0.0).astype(F32)
+    has_below = jnp.where(sp < SP - 1, 1.0, 0.0).astype(F32)
+    edge = lax.broadcasted_iota(jnp.int32, (EB, X), 0)
+    for f in range(F):
+        up = halo_v[0, f:f + 1, :] * ((DIFF + settling[f]) * has_above)
+        rb_v[f * R:f * R + EB, :] = (er_v[0, f] + jnp.where(edge == 0, up, 0.0)).astype(BF16)
+        low = halo_v[1, f:f + 1, :] * (DIFF * has_below)
+        rb_v[(f + 1) * R - EB:(f + 1) * R, :] = (
+            er_v[1, f] + jnp.where(edge == EB - 1, low, 0.0)
+        ).astype(BF16)
 
     keep = jnp.where(t < 2 * CHIPS - 1, 1.0, 0.0).astype(F32)
     sigma = jnp.where(z == 0, ALPHA, 1.0).astype(F32)
@@ -162,11 +174,11 @@
             if d and i == 0:
                 gather(d, 0).start()
 
-    third(chip(ORDER[0]))
-    for prev, d in zip(ORDER[:-1], ORDER[1:]):
-        third(chip(d))
-        partial(prev)
-    partial(ORDER[-1])
+    for n in range(CHIPS + AHEAD):
+        if n < CHIPS:
+            third(chip(ORDER[n]))
+        if n >= AHEAD:
+            partial(ORDER[n - AHEAD])
     for i in range(1, H):
         for d in ORDER[:-1]:
             gather(d, i).start()
@@ -239,9 +251,6 @@
         finish(prev, c_v if prev == 0 else acc_v)
     finish(arrive[-1], acc_v)
 
-    store = pltpu.make_async_copy(acc_v, out_h, o_sem)
-    store.start()
-
     for k in range(CHIPS):
         swap_a(k).wait_send()
         for i in range(H):
@@ -250,21 +259,20 @@
         for i in range(H):
             gather(d, i).wait_send()
             give(d, i).wait_send()
-    store.wait()
 
 
 def on_device(c, f, e, lam, table, cls, bed):
     F, S, R, X = c.shape
     SP = lax.axis_size("space")
     TN, H, M = X // CHIPS, F // 2, F * R
-    any_spec = pl.BlockSpec(memory_space=pl.ANY)
+    any_spec = pl.BlockSpec(memory_space=pltpu.HBM)
     smem_spec = pl.BlockSpec(memory_space=pltpu.SMEM)
     dma = pltpu.SemaphoreType.DMA
     out = pl.pallas_call(
         functools.partial(kernel, F, R, X, SP),
         out_shape=jax.ShapeDtypeStruct((M, X), F32),
         in_specs=[smem_spec, smem_spec] + [any_spec] * 5,
-        out_specs=any_spec,
+        out_specs=pl.BlockSpec(memory_space=pltpu.VMEM),
         scratch_shapes=[
             pltpu.VMEM((M, X), F32),
             pltpu.VMEM((M, X), F32),
@@ -277,6 +285,7 @@
             pltpu.VMEM((M, X), BF16),
             pltpu.VMEM((2, F, X), F32),
             pltpu.VMEM((2, F, X), F32),
+            pltpu.VMEM((2, F, EB, X), F32),
             pltpu.VMEM((F, CHIPS, 1, TN), F32),
             pltpu.VMEM((CHIPS, F, R, TN), F32),
             pltpu.VMEM((CHIPS, H, R, TN), F32),
@@ -286,7 +295,6 @@
             pltpu.VMEM((CHIPS, H, R, TN), BF16),
             pltpu.VMEM((CHIPS, H, R, TN), F32),
             pltpu.VMEM((CHIPS, F, R, TN), F32),
-            pltpu.VMEM((M, X), F32),
             dma((4,)),
             dma((CHIPS,)),
             dma((2,)), dma((2,)),
@@ -294,10 +302,9 @@
             dma((CHIPS, H)), dma((CHIPS, H)),
             dma((CHIPS, H)), dma((CHIPS, H)),
             dma((CHIPS, H)), dma((CHIPS, H)),
-            dma,
         ],
         compiler_params=pltpu.CompilerParams(
-            collective_id=0, has_side_effects=True, vmem_limit_bytes=60 * 1024 * 1024
+            collective_id=0, has_side_effects=True, vmem_limit_bytes=57 * 1024 * 1024
         ),
     )(
         table, cls, c.reshape(M, X), f.reshape(M, X), e, lam.reshape(1, X), bed,

time: 65.5 us -> 58.4 us (0.89)
  Pallas kernels: 62.3 us -> 55.1 us
    pallas_call x1, Pallas kernels: 62.3 us -> 55.1 us  [on_device(): pl.pallas_call(functools.partial(kernel, F, R, X, SP), out_shape=jax.Shap...]
where the time goes in v3:
time: 58.4 us; the launch traced here: 58.3 us
  Pallas kernels  55.1 us (94%)
  local copies, waits for them, and re-layouts  3.14 us (5%)
    pallas_call x1, Pallas kernels, on_device(): pl.pallas_call(functools.partial(kernel, F, R, X, SP), out_shape=jax.Shap...  55.1 us
    unnamed x1, local copies, waits for them, and re-layouts  3.14 us

profile of v3, /device:TPU:1, one launch (start us, length us, event | category | flops | bytes accessed | tf_op | source)
XLA Modules:
  0.0 58.3 jit_solution(10130118826426409717)
XLA Ops:
  0.0 55.1 %shard_map.73 = f32[256,2048]{1,0:T(8,128)} custom-call(f32[8]{0:T(128)} %table_s.1, s32[4]{0:T(128)} %class_s.1, f32[256,2048]{1,0:T(8,128)} %bitcast.7, f32[256,2048]{1,0:T(8,128)} %bitcast.8, bf16[2048,2048]{1,0:T(8,128)(2,1)} %e_h.1, f32[1,2048]{1,0:T(1,128)} %bitcast.9, s32[64,2048]{1,0:T(8,128)} %bed_h.1), custom_call_target="tpu_custom_call" | custom-call | tf_op jit(solution)/shard_map/pallas_call | solution.py:271
  55.1 3.1 %copy.10 = f32[4,1,64,2048]{3,2,1,0:T(8,128)} copy(f32[4,1,64,2048]{3,2,1,0:T(8,128)} %bitcast.6) | data formatting | bytes 4194304

commit v4 on v3

v4 whole, which is shorter than its diff:
```python
import functools

import jax
import jax.numpy as jnp
from jax import lax
from jax.experimental import pallas as pl
from jax.experimental.pallas import tpu as pltpu
from jax.sharding import PartitionSpec as P

ALPHA = 0.5
DIFF = 0.06
DEPO = 0.1
MESH = pl.DeviceIdType.MESH
ORDER = (4, 3, 5, 2, 6, 1, 7, 0)
CHIPS = 8
EARLY = 2
AHEAD = 2
F32, BF16 = jnp.float32, jnp.bfloat16


def PIECES(R):
    edge = R // 4
    return (0, edge, 2 * edge, 0), (1, 0, edge, 0), (1, R - edge, edge, edge)


def nt(a, b):
    return lax.dot_general(a, b, (((1,), (1,)), ((), ())), preferred_element_type=F32)


def nn(a, b):
    return jnp.dot(a, b, preferred_element_type=F32)


def kernel(
    F, R, X, SP,
    table_s, class_s, c_h, f_h, e_h, lam_h, bed_h, acc_v,
    c_v, f_v, e_v, lam_v, bed_v, cb_v, q_v, cp_v, rb_v, edge_v, halo_v, dinv_v,
    a_v, ar_v, xs_v, xr_v, ys_v, yr_v, zs_v, wz_v,
    ld, e_sem, h_ss, h_rs, a_ss, a_rs, g_ss, g_rs, s_ss, s_rs, z_ss, z_rs,
):
    TN = X // CHIPS
    H = F // 2
    RG, EB = R // 2, R // 4
    MG = F * RG
    t = lax.axis_index("tm")
    sp = lax.axis_index("space")
    z, h = t // 2, t % 2
    partner = (z * 2 + 1 - h, sp)
    below = (t, (sp + 1) % SP)
    above = (t, (sp + SP - 1) % SP)

    def cols(j):
        return pl.ds(pl.multiple_of(j * TN, TN), TN)

    def load_e(j):
        return pltpu.make_async_copy(e_h.at[:, cols(j)], e_v.at[:, cols(j)], e_sem.at[j])

    ld_c = pltpu.make_async_copy(c_h, c_v, ld.at[0])
    ld_l = pltpu.make_async_copy(lam_h, lam_v, ld.at[1])
    ld_f = pltpu.make_async_copy(f_h, f_v, ld.at[2])
    ld_b = pltpu.make_async_copy(bed_h, bed_v, ld.at[3])
    barrier = pltpu.get_barrier_semaphore()
    rest = [(((z + d) % CHIPS) * 2 + h, sp) for d in range(1, CHIPS)]
    for dev in [partner, below, above] + rest:
        pl.semaphore_signal(barrier, inc=1, device_id=dev, device_id_type=MESH)

    ld_c.start()
    ld_l.start()
    for j in range(CHIPS):
        load_e(j).start()
    ld_f.start()
    ld_b.start()

    ld_l.wait()
    settling = [table_s[class_s[f]] for f in range(F)]
    for j in range(CHIPS):
        for f in range(F):
            dinv_v[f, j] = 1.0 / (1.0 + 2.0 * DIFF + settling[f] - lam_v[:, j * TN:(j + 1) * TN])

    ld_c.wait()
    for f in range(F):
        for g, src, n, off in PIECES(R):
            dst = g * MG + f * RG + off
            cb_v[dst:dst + n, :] = c_v[f * R + src:f * R + src + n, :].astype(BF16)
        edge_v[0, f:f + 1, :] = c_v[(f + 1) * R - 1:(f + 1) * R, :]
        edge_v[1, f:f + 1, :] = c_v[f * R:f * R + 1, :]

    def first(j, carry):
        load_e(j).wait()
        q = nn(cb_v[...], e_v[:, cols(j)])
        q_v[j] = q
        cp_v[:, cols(j)] = (q * lam_v[:, cols(j)]).astype(BF16)
        return carry

    def halo(i, dev):
        return pltpu.make_async_remote_copy(
            edge_v.at[i], halo_v.at[i], h_ss.at[i], h_rs.at[i], device_id=dev, device_id_type=MESH
        )

    lax.fori_loop(0, EARLY, first, 0)
    pl.semaphore_wait(barrier, CHIPS + 2)
    halo(0, below).start()
    halo(1, above).start()
    lax.fori_loop(EARLY, CHIPS, first, 0)
    ld_f.wait()
    ld_b.wait()

    has_above = jnp.where(sp > 0, 1.0, 0.0).astype(F32)
    has_below = jnp.where(sp < SP - 1, 1.0, 0.0).astype(F32)

    def second(g):
        def tile(j, carry):
            along = nt(cp_v[g * MG:(g + 1) * MG, :], e_v[cols(j), :])
            for f in range(F):
                for piece, src, n, off in PIECES(R):
                    if piece != g:
                        continue
                    lo, hi = max(src - 8, 0), min(src + n + 8, R)
                    wide = c_v[f * R + lo:f * R + hi, cols(j)]
                    inner = slice(src - lo, src - lo + n)
                    c = wide[inner]
                    up = pltpu.roll(wide, 1, 0)[inner]
                    low = pltpu.roll(wide, hi - lo - 1, 0)[inner]
                    row = lax.broadcasted_iota(jnp.int32, (n, TN), 0)
                    if src == 0:
                        up = jnp.where(row == 0, halo_v[0, f:f + 1, cols(j)] * has_above, up)
                    if src + n == R:
                        low = jnp.where(row == n - 1, halo_v[1, f:f + 1, cols(j)] * has_below, low)
                    bed = DEPO * bed_v[src:src + n, cols(j)].astype(F32)
                    vert = DIFF * (low - 2.0 * c + up) + settling[f] * (up - c) - bed * c
                    dst = g * MG + f * RG + off
                    kept = c - cb_v[dst:dst + n, cols(j)].astype(F32)
                    rest = f_v[f * R + src:f * R + src + n, cols(j)] - kept + vert
                    rest = rest + along[f * RG + off:f * RG + off + n]
                    rb_v[dst:dst + n, cols(j)] = rest.astype(BF16)
            return carry

        lax.fori_loop(0, CHIPS, tile, 0)

    keep = jnp.where(t < 2 * CHIPS - 1, 1.0, 0.0).astype(F32)
    sigma = jnp.where(z == 0, ALPHA, 1.0).astype(F32)

    def swap_a(g, k):
        return pltpu.make_async_remote_copy(
            a_v.at[k, g, pl.ds(H * (1 - h), H)], ar_v.at[k, g], a_ss.at[k, g], a_rs.at[k, g],
            device_id=partner, device_id_type=MESH,
        )

    def third(g, k):
        m = nn(rb_v[g * MG:(g + 1) * MG, :], e_v[:, cols(k)])
        for f in range(F):
            q = q_v[k, g * MG + f * RG:g * MG + (f + 1) * RG, :]
            a_v[k, g, f] = (m[f * RG:(f + 1) * RG] - q) * dinv_v[f, k] + keep * q
        swap_a(g, k).start()

    def chip(d):
        return (z + d) % CHIPS

    def gather(d, g):
        return pltpu.make_async_remote_copy(
            xs_v.at[d, g], xr_v.at[d, g], g_ss.at[d, g], g_rs.at[d, g],
            device_id=(chip(d) * 2 + h, sp), device_id_type=MESH,
        )

    def give(d, g):
        return pltpu.make_async_remote_copy(
            ys_v.at[d, g], yr_v.at[d, g], s_ss.at[d, g], s_rs.at[d, g],
            device_id=(chip(d) * 2 + h, sp), device_id_type=MESH,
        )

    def pair(g, k, i):
        own, other = a_v[k, g, H * h + i], ar_v[k, g, i]
        return jnp.where(h == 0, own, other), jnp.where(h == 0, other, own)

    def partial(g, d):
        k = chip(d)
        swap_a(g, k).wait_recv()
        for i in range(H):
            a0, a1 = pair(g, k, i)
            xs_v[d, g, i] = (a1 + dinv_v[H * h + i, k] * a0).astype(BF16)
        if d:
            gather(d, g).start()

    def send(g):
        second(g)
        for n in range(CHIPS + AHEAD):
            if n < CHIPS:
                third(g, chip(ORDER[n]))
            if n >= AHEAD:
                partial(g, ORDER[n - AHEAD])

    send(0)
    halo(0, below).wait()
    halo(1, above).wait()
    send(1)

    def solve(g):
        for d in ORDER[:-1]:
            gather(d, g).wait_recv()
        xr_v[0, g] = xs_v[0, g]
        for i in range(H):
            d1 = dinv_v[H * h + i, z]
            d2 = d1 * d1
            d4 = d2 * d2
            d8 = d4 * d4

            def part(c):
                return xr_v[(z - c + CHIPS) % CHIPS, g, i].astype(F32)

            total = part(0)
            for c in range(1, CHIPS):
                total = part(c) + d2 * total
            state = total / (1.0 - ALPHA * (d8 * d8))
            for c in range(CHIPS):
                ys_v[(c - z + CHIPS) % CHIPS, g, i] = state.astype(BF16)
                state = part(c) + d2 * (state * ALPHA if c == 0 else state)
        for d in ORDER[:-1]:
            give(d, g).start()
        yr_v[0, g] = ys_v[0, g]

    solve(0)
    solve(1)

    def swap_z(g, k):
        return pltpu.make_async_remote_copy(
            zs_v.at[k, g], wz_v.at[k, g, pl.ds(H * h, H)], z_ss.at[k, g], z_rs.at[k, g],
            device_id=partner, device_id_type=MESH,
        )

    def stage(g, d):
        k = (z - d + CHIPS) % CHIPS
        if d:
            give(d, g).wait_recv()
        for i in range(H):
            a0, a1 = pair(g, k, i)
            d1 = dinv_v[H * h + i, k]
            z0 = a0 + (sigma * d1) * yr_v[d, g, i].astype(F32)
            z1 = a1 + d1 * z0
            zs_v[k, g, i] = jnp.where(h == 0, z1, z0)
            wz_v[k, g, H * h + i] = jnp.where(h == 0, z0, z1)
        swap_z(g, k).start()

    def finish(d, base):
        k = (z - d + CHIPS) % CHIPS
        for g in range(2):
            swap_z(g, k).wait_recv()
        blocks = []
        for f in range(F):
            w = [
                wz_v[k, g, f] - keep * q_v[k, g * MG + f * RG:g * MG + (f + 1) * RG, :]
                for g in range(2)
            ]
            blocks += [w[1][:EB], w[0], w[1][EB:]]
        w = jnp.concatenate(blocks, axis=0).astype(BF16)
        step = 2 * TN

        def part(n, carry):
            cs = pl.ds(pl.multiple_of(n * step, step), step)
            acc_v[:, cs] = base[:, cs] + nt(w, e_v[cs, cols(k)])
            return carry

        lax.fori_loop(0, X // step, part, 0)

    arrive = (0,) + ORDER[:-1]
    for d in arrive:
        stage(0, d)
    stage(1, arrive[0])
    for prev, d in zip(arrive[:-1], arrive[1:]):
        stage(1, d)
        finish(prev, c_v if prev == 0 else acc_v)
    finish(arrive[-1], acc_v)

    for g in range(2):
        for k in range(CHIPS):
            swap_a(g, k).wait_send()
            swap_z(g, k).wait_send()
        for d in ORDER[:-1]:
            gather(d, g).wait_send()
            give(d, g).wait_send()


def on_device(c, f, e, lam, table, cls, bed):
    F, S, R, X = c.shape
    SP = lax.axis_size("space")
    TN, H, M = X // CHIPS, F // 2, F * R
    any_spec = pl.BlockSpec(memory_space=pltpu.HBM)
    smem_spec = pl.BlockSpec(memory_space=pltpu.SMEM)
    dma = pltpu.SemaphoreType.DMA
    out = pl.pallas_call(
        functools.partial(kernel, F, R, X, SP),
        out_shape=jax.ShapeDtypeStruct((M, X), F32),
        in_specs=[smem_spec, smem_spec] + [any_spec] * 5,
        out_specs=pl.BlockSpec(memory_space=pltpu.VMEM),
        scratch_shapes=[
            pltpu.VMEM((M, X), F32),
            pltpu.VMEM((M, X), F32),
            pltpu.VMEM((X, X), BF16),
            pltpu.VMEM((1, X), F32),
            pltpu.VMEM((R, X), jnp.int32),
            pltpu.VMEM((M, X), BF16),
            pltpu.VMEM((CHIPS, M, TN), F32),
            pltpu.VMEM((M, X), BF16),
            pltpu.VMEM((M, X), BF16),
            pltpu.VMEM((2, F, X), F32),
            pltpu.VMEM((2, F, X), F32),
            pltpu.VMEM((F, CHIPS, 1, TN), F32),
            pltpu.VMEM((CHIPS, 2, F, R // 2, TN), F32),
            pltpu.VMEM((CHIPS, 2, H, R // 2, TN), F32),
            pltpu.VMEM((CHIPS, 2, H, R // 2, TN), BF16),
            pltpu.VMEM((CHIPS, 2, H, R // 2, TN), BF16),
            pltpu.VMEM((CHIPS, 2, H, R // 2, TN), BF16),
            pltpu.VMEM((CHIPS, 2, H, R // 2, TN), BF16),
            pltpu.VMEM((CHIPS, 2, H, R // 2, TN), F32),
            pltpu.VMEM((CHIPS, 2, F, R // 2, TN), F32),
            dma((4,)),
            dma((CHIPS,)),
            dma((2,)), dma((2,)),
            dma((CHIPS, 2)), dma((CHIPS, 2)),
            dma((CHIPS, 2)), dma((CHIPS, 2)),
            dma((CHIPS, 2)), dma((CHIPS, 2)),
            dma((CHIPS, 2)), dma((CHIPS, 2)),
        ],
        compiler_params=pltpu.CompilerParams(
            collective_id=0, has_side_effects=True, vmem_limit_bytes=57 * 1024 * 1024
        ),
    )(
        table, cls, c.reshape(M, X), f.reshape(M, X), e, lam.reshape(1, X), bed,
    )
    return out.reshape(F, S, R, X)


def solution(mesh):
    return jax.shard_map(
        on_device,
        mesh=mesh,
        in_specs=(
            P(None, "tm", "space", None),
            P(None, "tm", "space", None),
            P(),
            P(),
            P(),
            P(),
            P("space", None),
        ),
        out_specs=P(None, "tm", "space", None),
        check_vma=False,
    )
```

time: 58.4 us -> 60.9 us (1.043)
  Pallas kernels: 55.1 us -> 57.6 us
    pallas_call x1, Pallas kernels: 55.1 us -> 57.6 us  [on_device(): pl.pallas_call(functools.partial(kernel, F, R, X, SP), out_shape=jax.Shap...]
where the time goes in v4:
time: 60.9 us; the launch traced here: 60.8 us
  Pallas kernels  57.6 us (95%)
  local copies, waits for them, and re-layouts  3.14 us (5%)
    pallas_call x1, Pallas kernels, on_device(): pl.pallas_call(functools.partial(kernel, F, R, X, SP), out_shape=jax.Shap...  57.6 us
    unnamed x1, local copies, waits for them, and re-layouts  3.14 us

profile of v4, /device:TPU:1, one launch (start us, length us, event | category | flops | bytes accessed | tf_op | source)
XLA Modules:
  0.0 60.8 jit_solution(11993466093924154005)
XLA Ops:
  0.0 57.6 %shard_map.73 = f32[256,2048]{1,0:T(8,128)} custom-call(f32[8]{0:T(128)} %table_s.1, s32[4]{0:T(128)} %class_s.1, f32[256,2048]{1,0:T(8,128)} %bitcast.7, f32[256,2048]{1,0:T(8,128)} %bitcast.8, bf16[2048,2048]{1,0:T(8,128)(2,1)} %e_h.1, f32[1,2048]{1,0:T(1,128)} %bitcast.9, s32[64,2048]{1,0:T(8,128)} %bed_h.1), custom_call_target="tpu_custom_call" | custom-call | tf_op jit(solution)/shard_map/pallas_call | solution.py:289
  57.7 3.1 %copy.10 = f32[4,1,64,2048]{3,2,1,0:T(8,128)} copy(f32[4,1,64,2048]{3,2,1,0:T(8,128)} %bitcast.6) | data formatting | bytes 4194304

commit v5 on v4

--- a/solution.py
+++ b/solution.py
@@ -12,6 +12,7 @@
 DEPO = 0.1
 MESH = pl.DeviceIdType.MESH
 ORDER = (4, 3, 5, 2, 6, 1, 7, 0)
+NEAR = (1, 7, 2, 6, 3, 5, 4)
 CHIPS = 8
 EARLY = 2
 AHEAD = 2
@@ -34,7 +35,7 @@
 def kernel(
     F, R, X, SP,
     table_s, class_s, c_h, f_h, e_h, lam_h, bed_h, acc_v,
-    c_v, f_v, e_v, lam_v, bed_v, cb_v, q_v, cp_v, rb_v, edge_v, halo_v, dinv_v,
+    c_v, f_v, e_v, lam_v, bed_v, cb_v, q_v, cp_v, rb_v, edge_v, halo_v, hr_v, dinv_v,
     a_v, ar_v, xs_v, xr_v, ys_v, yr_v, zs_v, wz_v,
     ld, e_sem, h_ss, h_rs, a_ss, a_rs, g_ss, g_rs, s_ss, s_rs, z_ss, z_rs,
 ):
@@ -105,37 +106,30 @@
     ld_f.wait()
     ld_b.wait()
 
-    has_above = jnp.where(sp > 0, 1.0, 0.0).astype(F32)
-    has_below = jnp.where(sp < SP - 1, 1.0, 0.0).astype(F32)
-
-    def second(g):
-        def tile(j, carry):
-            along = nt(cp_v[g * MG:(g + 1) * MG, :], e_v[cols(j), :])
-            for f in range(F):
-                for piece, src, n, off in PIECES(R):
-                    if piece != g:
-                        continue
-                    lo, hi = max(src - 8, 0), min(src + n + 8, R)
-                    wide = c_v[f * R + lo:f * R + hi, cols(j)]
-                    inner = slice(src - lo, src - lo + n)
-                    c = wide[inner]
-                    up = pltpu.roll(wide, 1, 0)[inner]
-                    low = pltpu.roll(wide, hi - lo - 1, 0)[inner]
-                    row = lax.broadcasted_iota(jnp.int32, (n, TN), 0)
-                    if src == 0:
-                        up = jnp.where(row == 0, halo_v[0, f:f + 1, cols(j)] * has_above, up)
-                    if src + n == R:
-                        low = jnp.where(row == n - 1, halo_v[1, f:f + 1, cols(j)] * has_below, low)
-                    bed = DEPO * bed_v[src:src + n, cols(j)].astype(F32)
-                    vert = DIFF * (low - 2.0 * c + up) + settling[f] * (up - c) - bed * c
-                    dst = g * MG + f * RG + off
-                    kept = c - cb_v[dst:dst + n, cols(j)].astype(F32)
-                    rest = f_v[f * R + src:f * R + src + n, cols(j)] - kept + vert
-                    rest = rest + along[f * RG + off:f * RG + off + n]
-                    rb_v[dst:dst + n, cols(j)] = rest.astype(BF16)
-            return carry
-
-        lax.fori_loop(0, CHIPS, tile, 0)
+    def second(j, carry):
+        along = nt(cp_v[...], e_v[cols(j), :])
+        for f in range(F):
+            for g, src, n, off in PIECES(R):
+                lo, hi = max(src - 8, 0), min(src + n + 8, R)
+                wide = c_v[f * R + lo:f * R + hi, cols(j)]
+                inner = slice(src - lo, src - lo + n)
+                c = wide[inner]
+                up = pltpu.roll(wide, 1, 0)[inner]
+                low = pltpu.roll(wide, hi - lo - 1, 0)[inner]
+                row = lax.broadcasted_iota(jnp.int32, (n, TN), 0)
+                if src == 0:
+                    up = jnp.where(row == 0, 0.0, up)
+                if src + n == R:
+                    low = jnp.where(row == n - 1, 0.0, low)
+                bed = DEPO * bed_v[src:src + n, cols(j)].astype(F32)
+                vert = DIFF * (low - 2.0 * c + up) + settling[f] * (up - c) - bed * c
+                dst = g * MG + f * RG + off
+                kept = c - cb_v[dst:dst + n, cols(j)].astype(F32)
+                rest = f_v[f * R + src:f * R + src + n, cols(j)] - kept + vert
+                rb_v[dst:dst + n, cols(j)] = (rest + along[dst:dst + n]).astype(BF16)
+        return carry
+
+    lax.fori_loop(0, CHIPS, second, 0)
 
     keep = jnp.where(t < 2 * CHIPS - 1, 1.0, 0.0).astype(F32)
     sigma = jnp.where(z == 0, ALPHA, 1.0).astype(F32)
@@ -146,12 +140,24 @@
             device_id=partner, device_id_type=MESH,
         )
 
-    def third(g, k):
-        m = nn(rb_v[g * MG:(g + 1) * MG, :], e_v[:, cols(k)])
+    def third(k):
+        m = nn(rb_v[...], e_v[:, cols(k)])
+        for g in range(2):
+            for f in range(F):
+                rows = slice(g * MG + f * RG, g * MG + (f + 1) * RG)
+                q = q_v[k, rows, :]
+                a_v[k, g, f] = (m[rows] - q) * dinv_v[f, k] + keep * q
+        swap_a(0, k).start()
+
+    def add_halo(k):
+        m = nn(hr_v[...], e_v[:, cols(k)])
+        row = lax.broadcasted_iota(jnp.int32, (8, TN), 0)
         for f in range(F):
-            q = q_v[k, g * MG + f * RG:g * MG + (f + 1) * RG, :]
-            a_v[k, g, f] = (m[f * RG:(f + 1) * RG] - q) * dinv_v[f, k] + keep * q
-        swap_a(g, k).start()
+            up = m[f:f + 1] * dinv_v[f, k]
+            low = m[F + f:F + f + 1] * dinv_v[f, k]
+            a_v[k, 1, f, 0:8] = a_v[k, 1, f, 0:8] + jnp.where(row == 0, up, 0.0)
+            a_v[k, 1, f, RG - 8:RG] = a_v[k, 1, f, RG - 8:RG] + jnp.where(row == 7, low, 0.0)
+        swap_a(1, k).start()
 
     def chip(d):
         return (z + d) % CHIPS
@@ -181,18 +187,26 @@
         if d:
             gather(d, g).start()
 
-    def send(g):
-        second(g)
+    def send(g, make):
         for n in range(CHIPS + AHEAD):
             if n < CHIPS:
-                third(g, chip(ORDER[n]))
+                make(chip(ORDER[n]))
             if n >= AHEAD:
                 partial(g, ORDER[n - AHEAD])
 
-    send(0)
+    send(0, third)
     halo(0, below).wait()
     halo(1, above).wait()
-    send(1)
+    has_above = jnp.where(sp > 0, 1.0, 0.0).astype(F32)
+    has_below = jnp.where(sp < SP - 1, 1.0, 0.0).astype(F32)
+    row = lax.broadcasted_iota(jnp.int32, (16, X), 0)
+    edges = jnp.zeros((16, X), F32)
+    for f in range(F):
+        up = halo_v[0, f:f + 1, :] * ((DIFF + settling[f]) * has_above)
+        low = halo_v[1, f:f + 1, :] * (DIFF * has_below)
+        edges = jnp.where(row == f, up, jnp.where(row == F + f, low, edges))
+    hr_v[...] = edges.astype(BF16)
+    send(1, add_halo)
 
     def solve(g):
         for d in ORDER[:-1]:
@@ -214,7 +228,7 @@
             for c in range(CHIPS):
                 ys_v[(c - z + CHIPS) % CHIPS, g, i] = state.astype(BF16)
                 state = part(c) + d2 * (state * ALPHA if c == 0 else state)
-        for d in ORDER[:-1]:
+        for d in NEAR:
             give(d, g).start()
         yr_v[0, g] = ys_v[0, g]
 
@@ -261,7 +275,7 @@
 
         lax.fori_loop(0, X // step, part, 0)
 
-    arrive = (0,) + ORDER[:-1]
+    arrive = (0,) + NEAR
     for d in arrive:
         stage(0, d)
     stage(1, arrive[0])
@@ -303,6 +317,7 @@
             pltpu.VMEM((M, X), BF16),
             pltpu.VMEM((2, F, X), F32),
             pltpu.VMEM((2, F, X), F32),
+            pltpu.VMEM((16, X), BF16),
             pltpu.VMEM((F, CHIPS, 1, TN), F32),
             pltpu.VMEM((CHIPS, 2, F, R // 2, TN), F32),
             pltpu.VMEM((CHIPS, 2, H, R // 2, TN), F32),

time: 60.9 us -> 57.4 us (0.943)
  Pallas kernels: 57.6 us -> 54.1 us
    pallas_call x1, Pallas kernels: 57.6 us -> 54.1 us  [on_device(): pl.pallas_call(functools.partial(kernel, F, R, X, SP), out_shape=jax.Shap...]
where the time goes in v5:
time: 57.4 us; the launch traced here: 57.3 us
  Pallas kernels  54.1 us (94%)
  local copies, waits for them, and re-layouts  3.14 us (5%)
    pallas_call x1, Pallas kernels, on_device(): pl.pallas_call(functools.partial(kernel, F, R, X, SP), out_shape=jax.Shap...  54.1 us
    unnamed x1, local copies, waits for them, and re-layouts  3.14 us

profile of v5, /device:TPU:1, one launch (start us, length us, event | category | flops | bytes accessed | tf_op | source)
XLA Modules:
  0.0 57.3 jit_solution(12441657659607808306)
XLA Ops:
  0.0 54.1 %shard_map.73 = f32[256,2048]{1,0:T(8,128)} custom-call(f32[8]{0:T(128)} %table_s.1, s32[4]{0:T(128)} %class_s.1, f32[256,2048]{1,0:T(8,128)} %bitcast.7, f32[256,2048]{1,0:T(8,128)} %bitcast.8, bf16[2048,2048]{1,0:T(8,128)(2,1)} %e_h.1, f32[1,2048]{1,0:T(1,128)} %bitcast.9, s32[64,2048]{1,0:T(8,128)} %bed_h.1), custom_call_target="tpu_custom_call" | custom-call | tf_op jit(solution)/shard_map/pallas_call | solution.py:303
  54.1 3.1 %copy.10 = f32[4,1,64,2048]{3,2,1,0:T(8,128)} copy(f32[4,1,64,2048]{3,2,1,0:T(8,128)} %bitcast.6) | data formatting | bytes 4194304

commit v6 on v5

--- a/solution.py
+++ b/solution.py
@@ -13,6 +13,7 @@
 MESH = pl.DeviceIdType.MESH
 ORDER = (4, 3, 5, 2, 6, 1, 7, 0)
 NEAR = (1, 7, 2, 6, 3, 5, 4)
+GROUPS = ((0, 1, 7, 2), (6, 3, 5, 4))
 CHIPS = 8
 EARLY = 2
 AHEAD = 2
@@ -34,10 +35,10 @@
 
 def kernel(
     F, R, X, SP,
-    table_s, class_s, c_h, f_h, e_h, lam_h, bed_h, acc_v,
+    table_s, class_s, c_h, f_h, e_h, lam_h, bed_h, out_h,
     c_v, f_v, e_v, lam_v, bed_v, cb_v, q_v, cp_v, rb_v, edge_v, halo_v, hr_v, dinv_v,
-    a_v, ar_v, xs_v, xr_v, ys_v, yr_v, zs_v, wz_v,
-    ld, e_sem, h_ss, h_rs, a_ss, a_rs, g_ss, g_rs, s_ss, s_rs, z_ss, z_rs,
+    a_v, ar_v, xs_v, xr_v, ys_v, yr_v, zs_v, wz_v, w_v, acc_v,
+    ld, e_sem, h_ss, h_rs, a_ss, a_rs, g_ss, g_rs, s_ss, s_rs, z_ss, z_rs, o_sem,
 ):
     TN = X // CHIPS
     H = F // 2
@@ -254,7 +255,7 @@
             wz_v[k, g, H * h + i] = jnp.where(h == 0, z0, z1)
         swap_z(g, k).start()
 
-    def finish(d, base):
+    def ready(d):
         k = (z - d + CHIPS) % CHIPS
         for g in range(2):
             swap_z(g, k).wait_recv()
@@ -265,24 +266,38 @@
                 for g in range(2)
             ]
             blocks += [w[1][:EB], w[0], w[1][EB:]]
-        w = jnp.concatenate(blocks, axis=0).astype(BF16)
-        step = 2 * TN
+        w_v[d] = jnp.concatenate(blocks, axis=0).astype(BF16)
+
+    step = 2 * TN
+
+    def store(n):
+        cs = pl.ds(pl.multiple_of(n * step, step), step)
+        return pltpu.make_async_copy(acc_v.at[:, cs], out_h.at[:, cs], o_sem.at[n])
+
+    def product(ds, base, last):
 
         def part(n, carry):
             cs = pl.ds(pl.multiple_of(n * step, step), step)
-            acc_v[:, cs] = base[:, cs] + nt(w, e_v[cs, cols(k)])
+            total = base[:, cs]
+            for d in ds:
+                total = total + nt(w_v[d], e_v[cs, cols((z - d + CHIPS) % CHIPS)])
+            acc_v[:, cs] = total
+            if last:
+                store(n).start()
             return carry
 
         lax.fori_loop(0, X // step, part, 0)
 
-    arrive = (0,) + NEAR
-    for d in arrive:
+    for d in (0,) + NEAR:
         stage(0, d)
-    stage(1, arrive[0])
-    for prev, d in zip(arrive[:-1], arrive[1:]):
-        stage(1, d)
-        finish(prev, c_v if prev == 0 else acc_v)
-    finish(arrive[-1], acc_v)
+    base = c_v
+    for group in GROUPS:
+        for d in group:
+            stage(1, d)
+        for d in group:
+            ready(d)
+        product(group, base, group is GROUPS[-1])
+        base = acc_v
 
     for g in range(2):
         for k in range(CHIPS):
@@ -291,6 +306,8 @@
         for d in ORDER[:-1]:
             gather(d, g).wait_send()
             give(d, g).wait_send()
+    for n in range(CHIPS // 2):
+        store(n).wait()
 
 
 def on_device(c, f, e, lam, table, cls, bed):
@@ -304,7 +321,7 @@
         functools.partial(kernel, F, R, X, SP),
         out_shape=jax.ShapeDtypeStruct((M, X), F32),
         in_specs=[smem_spec, smem_spec] + [any_spec] * 5,
-        out_specs=pl.BlockSpec(memory_space=pltpu.VMEM),
+        out_specs=any_spec,
         scratch_shapes=[
             pltpu.VMEM((M, X), F32),
             pltpu.VMEM((M, X), F32),
@@ -327,6 +344,8 @@
             pltpu.VMEM((CHIPS, 2, H, R // 2, TN), BF16),
             pltpu.VMEM((CHIPS, 2, H, R // 2, TN), F32),
             pltpu.VMEM((CHIPS, 2, F, R // 2, TN), F32),
+            pltpu.VMEM((CHIPS, M, TN), BF16),
+            pltpu.VMEM((M, X), F32),
             dma((4,)),
             dma((CHIPS,)),
             dma((2,)), dma((2,)),
@@ -334,6 +353,7 @@
             dma((CHIPS, 2)), dma((CHIPS, 2)),
             dma((CHIPS, 2)), dma((CHIPS, 2)),
             dma((CHIPS, 2)), dma((CHIPS, 2)),
+            dma((CHIPS // 2,)),
         ],
         compiler_params=pltpu.CompilerParams(
             collective_id=0, has_side_effects=True, vmem_limit_bytes=57 * 1024 * 1024

time: 57.4 us -> 55.3 us (0.963)
  Pallas kernels: 54.1 us -> 52 us
    pallas_call x1, Pallas kernels: 54.1 us -> 52 us  [on_device(): pl.pallas_call(functools.partial(kernel, F, R, X, SP), out_shape=jax.Shap...]
where the time goes in v6:
time: 55.3 us; the launch traced here: 55.2 us
  Pallas kernels  52 us (94%)
  local copies, waits for them, and re-layouts  3.14 us (6%)
    pallas_call x1, Pallas kernels, on_device(): pl.pallas_call(functools.partial(kernel, F, R, X, SP), out_shape=jax.Shap...  52 us
    unnamed x1, local copies, waits for them, and re-layouts  3.14 us

profile of v6, /device:TPU:1, one launch (start us, length us, event | category | flops | bytes accessed | tf_op | source)
XLA Modules:
  0.0 55.2 jit_solution(9362771408800638063)
XLA Ops:
  0.0 52.0 %shard_map.73 = f32[256,2048]{1,0:T(8,128)} custom-call(f32[8]{0:T(128)} %table_s.1, s32[4]{0:T(128)} %class_s.1, f32[256,2048]{1,0:T(8,128)} %bitcast.7, f32[256,2048]{1,0:T(8,128)} %bitcast.8, bf16[2048,2048]{1,0:T(8,128)(2,1)} %e_h.1, f32[1,2048]{1,0:T(1,128)} %bitcast.9, s32[64,2048]{1,0:T(8,128)} %bed_h.1), custom_call_target="tpu_custom_call" | custom-call | tf_op jit(solution)/shard_map/pallas_call | solution.py:320
  52.1 3.1 %copy.10 = f32[4,1,64,2048]{3,2,1,0:T(8,128)} copy(f32[4,1,64,2048]{3,2,1,0:T(8,128)} %bitcast.6) | data formatting | bytes 4194304
